TPU v7x, 32 devices: a whole 2x2x4 slice. The times are simulated.
32 devices in a mesh: section: 2 (over x), dev: 16 (over z, y, core).
Axes of the slice: x: 2, y: 2, z: 4, core: 2. Of those that a mesh axis runs over, the one named last changes fastest.
Arguments:
- frames: bfloat16 [512, 32, 1024], P(('section', 'dev')), may hold values from -6 to 6
- window_counts: int32 [2, 16], replicated, may hold values from 1 to 20, 256 in all within a row
- learned_queries: bfloat16 [32, 1024], replicated, may hold values from -6 to 6
- frame_kv: bfloat16 [1024, 2048], replicated, may hold values from -0.1875 to 0.1875
- query_out: bfloat16 [1024, 1024], replicated, may hold values from -0.1875 to 0.1875
- query_gain: float32 [1024], replicated, may hold values from 0.25 to 1.75
- captions: bfloat16 [2, 16, 128, 2048], P('section', 'dev'), may hold values from -6 to 6
- caption_lengths: int32 [2, 16], P('section', 'dev'), may hold values from 1 to 128
- caption_gain: float32 [2048], replicated, may hold values from 0.25 to 1.75
- w_query: bfloat16 [2048, 1024], replicated, may hold values from -0.125 to 0.125
- memory_kv: bfloat16 [1024, 2048], replicated, may hold values from -0.1875 to 0.1875
- w_output: bfloat16 [1024, 2048], replicated, may hold values from -0.1875 to 0.1875
- upstream: bfloat16 [2, 16, 128, 2048], P('section', 'dev'), may hold values from -6 to 6
Outputs:
- decoded: bfloat16 [2, 16, 128, 2048], P('section', 'dev')
- caption_grad: bfloat16 [2, 16, 128, 2048], P('section', 'dev')
- memory_grad: bfloat16 [512, 32, 1024], P(('section', 'dev'))
- kv_grad: float32 [1024, 2048], P(('section', 'dev'))
Inputs may be any that keep to these rules, and one draw needn't show every extreme that they name: `window_counts`: each row sums to 256; in each row some video has exactly 20.
All inputs are finite; a program needn't handle non-finite values.
Results may differ from a plain program's by a relative error of at most 0.023.
Values may be sent and summed in bfloat16 or wider, within the bound.
A program may use at most 192 MiB of HBM per device.

v0:
```python
import jax
import jax.numpy as jnp
from jax import lax
from jax.experimental import pallas as pl
from jax.experimental.pallas import tpu as pltpu
from jax.sharding import PartitionSpec as P

HEAD_DIM = 64
MOST_WIN = 20
EPSILON = 1e-06
SCALE = HEAD_DIM ** (-0.5)
NT = (((1,), (1,)), ((), ()))
TN = (((0,), (0,)), ((), ()))
LANES = 128
VMEM = 60 * 1024 * 1024


def dot(a, b, dims=(((1,), (0,)), ((), ()))):
    return lax.dot_general(a, b, dims, preferred_element_type=jnp.float32)


def half_lanes(x, which):
    lane = lax.broadcasted_iota(jnp.int32, x.shape, 1)
    return jnp.where(lane // HEAD_DIM == which, x, jnp.zeros_like(x))


def compress_kernel(
    index_ref, frames_ref, queries_ref, kv_ref, out_w_ref, gain_ref, packed_ref, kv_s, ctx_s, mem_s
):
    step = pl.program_id(0)
    group, frames, width = frames_ref.shape
    tokens = queries_ref.shape[0]
    kv_s[...] = dot(frames_ref[...].reshape(group * frames, width), kv_ref[...]).astype(jnp.bfloat16)
    heads = 4
    span = heads * HEAD_DIM
    lane = lax.broadcasted_iota(jnp.int32, (tokens, span), 1) // HEAD_DIM
    for part in range(width // span):
        lo = part * span
        queries = queries_ref[:, lo : lo + span]
        stacked = jnp.concatenate(
            [jnp.where(lane == h, queries, jnp.zeros_like(queries)) for h in range(heads)], axis=0
        )
        scores = dot(kv_s[:, lo : lo + span], stacked, NT) * SCALE
        scores = scores.reshape(group, frames, heads * tokens)
        weights = jnp.exp(scores - jnp.max(scores, axis=1, keepdims=True))
        weights = (weights / jnp.sum(weights, axis=1, keepdims=True)).astype(jnp.bfloat16)
        for w in range(group):
            rows = slice(w * frames, (w + 1) * frames)
            every = dot(weights[w], kv_s[rows, width + lo : width + lo + span], TN)
            mixed = every[:tokens]
            for h in range(1, heads):
                mixed = jnp.where(lane == h, every[h * tokens : (h + 1) * tokens], mixed)
            ctx_s[w * tokens : (w + 1) * tokens, lo : lo + span] = mixed.astype(jnp.bfloat16)
    projected = dot(ctx_s[...], out_w_ref[...]).reshape(group, tokens, width)
    hidden = queries_ref[...].astype(jnp.float32)[None] + projected
    scale = lax.rsqrt(jnp.mean(hidden * hidden, axis=-1, keepdims=True) + EPSILON)
    mem_s[pl.ds(step * group, group)] = (hidden * scale * gain_ref[...][None]).astype(jnp.bfloat16)

    @pl.when(step == pl.num_programs(0) - 1)
    def _():
        def place(slot, carry):
            packed_ref[slot] = mem_s[index_ref[slot]]
            return carry

        lax.fori_loop(0, packed_ref.shape[0], place, 0)


def compress(index, frames, queries, frame_kv, query_out, gain):
    windows, length, width = frames.shape
    tokens = queries.shape[0]
    slots = index.shape[0]
    group = 8
    whole = lambda *shape: pl.BlockSpec(shape, lambda i, idx: (0,) * len(shape))
    return pl.pallas_call(
        compress_kernel,
        grid_spec=pltpu.PrefetchScalarGridSpec(
            num_scalar_prefetch=1,
            grid=(windows // group,),
            in_specs=[
                pl.BlockSpec((group, length, width), lambda i, idx: (i, 0, 0)),
                whole(tokens, width),
                whole(width, 2 * width),
                whole(width, width),
                whole(1, width),
            ],
            out_specs=whole(slots, tokens, width),
            scratch_shapes=[
                pltpu.VMEM((group * length, 2 * width), jnp.bfloat16),
                pltpu.VMEM((group * tokens, width), jnp.bfloat16),
                pltpu.VMEM((windows, tokens, width), jnp.bfloat16),
            ],
        ),
        out_shape=jax.ShapeDtypeStruct((slots, tokens, width), jnp.bfloat16),
        compiler_params=pltpu.CompilerParams(vmem_limit_bytes=48 * 1024 * 1024),
        cost_estimate=pl.CostEstimate(
            flops=2 * windows * length * width * width * 4,
            bytes_accessed=12 * 1024 * 1024,
            transcendentals=0,
        ),
        name="compress",
    )(index, frames, queries, frame_kv, query_out, gain.reshape(1, width))


def gather_kernel(index_ref, live_ref, table_ref, out_ref):
    def place(row, carry):
        value = table_ref[index_ref[row]]
        out_ref[row] = jnp.where(live_ref[row] > 0, value, jnp.zeros_like(value))
        return carry

    lax.fori_loop(0, out_ref.shape[0], place, 0)


def gather(index, live, table):
    rows = index.shape[0]
    shape = (rows,) + table.shape[1:]
    return pl.pallas_call(
        gather_kernel,
        grid_spec=pltpu.PrefetchScalarGridSpec(
            num_scalar_prefetch=2,
            grid=(1,),
            in_specs=[pl.BlockSpec(table.shape, lambda i, a, b: (0, 0, 0))],
            out_specs=pl.BlockSpec(shape, lambda i, a, b: (0, 0, 0)),
        ),
        out_shape=jax.ShapeDtypeStruct(shape, table.dtype),
        compiler_params=pltpu.CompilerParams(vmem_limit_bytes=24 * 1024 * 1024),
        name="gather",
    )(index, live, table)


def masked_scores(keys, queries, live):
    scores = dot(keys, queries, NT) * SCALE
    token = lax.broadcasted_iota(jnp.int32, scores.shape, 0)
    return jnp.where(token < live, scores, jnp.float32(-1e30))


def stats_kernel(live_ref, q_ref, g_ref, k_ref, v_ref, stats_ref):
    live = live_ref[0]
    rows = []
    for h in range(2):
        scores = masked_scores(k_ref[...], half_lanes(q_ref[...], h), live)
        most = jnp.max(scores, axis=0, keepdims=True)
        weights = jnp.exp(scores - most)
        d_probs = dot(v_ref[...], half_lanes(g_ref[...], h), NT)
        rows += [
            most,
            jnp.sum(weights, axis=0, keepdims=True),
            jnp.sum(weights * d_probs, axis=0, keepdims=True),
        ]
    rows += [jnp.zeros_like(rows[0])] * 2
    stats_ref[0] = jnp.concatenate(rows, axis=0)


def grads_kernel(
    live_ref, q_ref, g_ref, k_ref, v_ref, mine_ref, peer_ref, part_ref, d_kv_ref
):
    live = live_ref[0]
    mine, peer = mine_ref[0], peer_ref[0]
    keys, values = k_ref[...], v_ref[...]
    keys_t, values_t = keys.T, values.T
    d_keys = d_values = None
    d_query, context = [], []
    for h in range(2):
        queries, d_context = half_lanes(q_ref[...], h), half_lanes(g_ref[...], h)
        at = 3 * h
        most = jnp.maximum(mine[at : at + 1], peer[at : at + 1])
        scale_mine = jnp.exp(mine[at : at + 1] - most)
        scale_peer = jnp.exp(peer[at : at + 1] - most)
        inverse = 1.0 / (
            mine[at + 1 : at + 2] * scale_mine + peer[at + 1 : at + 2] * scale_peer
        )
        dots = (
            mine[at + 2 : at + 3] * scale_mine + peer[at + 2 : at + 3] * scale_peer
        ) * inverse
        probs = jnp.exp(masked_scores(keys, queries, live) - most) * inverse
        weights = probs.astype(jnp.bfloat16)
        d_probs = dot(values, d_context, NT)
        d_scores = (probs * (d_probs - dots) * SCALE).astype(jnp.bfloat16)
        cut = slice(h * HEAD_DIM, (h + 1) * HEAD_DIM)
        context.append(dot(values_t[cut], weights))
        d_query.append(dot(keys_t[cut], d_scores))
        dk, dv = dot(d_scores, queries), dot(weights, d_context)
        d_keys = dk if d_keys is None else d_keys + dk
        d_values = dv if d_values is None else d_values + dv
    part_ref[0] = jnp.concatenate(context, axis=0).T.astype(jnp.bfloat16)
    part_ref[1] = jnp.concatenate(d_query, axis=0).T.astype(jnp.bfloat16)
    d_kv_ref[0] = d_keys.astype(jnp.bfloat16)
    d_kv_ref[1] = d_values.astype(jnp.bfloat16)


def attention_specs(rows, keys, pairs):
    column = lambda n, shift: pl.BlockSpec((n, LANES), lambda i, live: (0, i + shift))
    return [column(rows, 0), column(rows, 0), column(keys, 0), column(keys, pairs)]


def attention_stats(live, q, g, kv):
    rows, width = q.shape
    pairs = width // LANES
    return pl.pallas_call(
        stats_kernel,
        grid_spec=pltpu.PrefetchScalarGridSpec(
            num_scalar_prefetch=1,
            grid=(pairs,),
            in_specs=attention_specs(rows, kv.shape[0], pairs),
            out_specs=pl.BlockSpec((1, 8, rows), lambda i, live: (i, 0, 0)),
        ),
        out_shape=jax.ShapeDtypeStruct((pairs, 8, rows), jnp.float32),
        compiler_params=pltpu.CompilerParams(vmem_limit_bytes=32 * 1024 * 1024),
        name="attention_stats",
    )(live, q, g, kv, kv)


def attention_grads(live, q, g, kv, mine, peer):
    rows, width = q.shape
    keys = kv.shape[0]
    pairs = width // LANES
    stats = pl.BlockSpec((1, 8, rows), lambda i, live: (i, 0, 0))
    return pl.pallas_call(
        grads_kernel,
        grid_spec=pltpu.PrefetchScalarGridSpec(
            num_scalar_prefetch=1,
            grid=(pairs,),
            in_specs=attention_specs(rows, keys, pairs) + [stats, stats],
            out_specs=[
                pl.BlockSpec((2, rows, LANES), lambda i, live: (0, 0, i)),
                pl.BlockSpec((2, keys, LANES), lambda i, live: (0, 0, i)),
            ],
        ),
        out_shape=[
            jax.ShapeDtypeStruct((2, rows, width), jnp.bfloat16),
            jax.ShapeDtypeStruct((2, keys, width), jnp.bfloat16),
        ],
        compiler_params=pltpu.CompilerParams(vmem_limit_bytes=32 * 1024 * 1024),
        name="attention_grads",
    )(live, q, g, kv, kv, mine, peer)


def swap(x):
    return lax.ppermute(x, "section", [(0, 1), (1, 0)])


def local(
    frames,
    window_counts,
    learned_queries,
    frame_kv,
    query_out,
    query_gain,
    captions,
    caption_lengths,
    caption_gain,
    w_query,
    memory_kv,
    w_output,
    upstream,
):
    videos = lax.axis_size("dev")
    windows, _, width = frames.shape
    tokens = learned_queries.shape[0]
    inner = w_query.shape[1]
    caplen = captions.shape[2]
    per_slot = (MOST_WIN + videos - 2) // (videos - 1)
    section_id = lax.axis_index("section")
    video_id = lax.axis_index("dev")
    counts_row = lax.dynamic_index_in_dim(window_counts, section_id, 0, keepdims=False)
    run_ends = jnp.cumsum(counts_row)
    starts = run_ends - counts_row
    local_index = jnp.arange(windows, dtype=jnp.int32)
    ranked = (
        local_index // per_slot * (per_slot * videos) + video_id * per_slot + local_index % per_slot
    )
    owner_video = jnp.sum((run_ends[None, :] <= ranked[:, None]).astype(jnp.int32), axis=1)
    target = owner_video * per_slot + local_index % per_slot
    slot_index = jnp.arange(videos * per_slot, dtype=jnp.int32)
    send_index = jnp.sum(
        jnp.where(slot_index[:, None] == target[None, :], local_index[None, :], 0), axis=1
    )
    count_here = lax.dynamic_index_in_dim(counts_row, video_id, 0, keepdims=False)
    start_here = lax.dynamic_index_in_dim(starts, video_id, 0, keepdims=False)
    position = jnp.arange(MOST_WIN, dtype=jnp.int32)
    incoming = start_here + position
    source_slot = incoming // per_slot % videos * per_slot + incoming % per_slot
    present = position < count_here
    return_index = jnp.sum(
        jnp.where(
            (slot_index[:, None] == source_slot[None, :]) & present[None, :], position[None, :], 0
        ),
        axis=1,
    )
    live = (count_here * tokens).reshape(1)

    x = captions[0, 0].astype(jnp.float32)
    inv_rms = lax.rsqrt(jnp.mean(x * x, axis=-1, keepdims=True) + EPSILON)
    normed = (x * inv_rms * caption_gain).astype(jnp.bfloat16)
    query = dot(normed, w_query).astype(jnp.bfloat16)
    row_live = jnp.arange(caplen, dtype=jnp.int32) < caption_lengths[0, 0]
    grad_out = jnp.where(row_live[:, None], upstream[0, 0], jnp.zeros_like(upstream[0, 0]))
    d_context = dot(grad_out, w_output, NT).astype(jnp.bfloat16)
    own = jnp.stack([query, d_context])
    both = jnp.concatenate([own, swap(own)], axis=1)

    packed = compress(send_index, frames, learned_queries, frame_kv, query_out, query_gain)
    arrived = lax.all_to_all(
        packed.reshape(videos, per_slot, tokens, width), "dev", split_axis=0, concat_axis=0, tiled=True
    ).reshape(videos * per_slot, tokens, width)
    memory_half = gather(source_slot, present.astype(jnp.int32), arrived).reshape(
        MOST_WIN * tokens, width
    )
    key_value = dot(memory_half, memory_kv).astype(jnp.bfloat16)

    stats = attention_stats(live, both[0], both[1], key_value)
    peer = swap(stats)
    peer = jnp.concatenate([peer[..., caplen:], peer[..., :caplen]], axis=-1)
    partial, d_kv = attention_grads(live, both[0], both[1], key_value, stats, peer)

    d_memory = (
        dot(d_kv[0], memory_kv[:, :inner], NT) + dot(d_kv[1], memory_kv[:, inner:], NT)
    ).astype(jnp.bfloat16)
    ones = jnp.ones_like(slot_index)
    grad_slots = gather(return_index, ones, d_memory.reshape(MOST_WIN, tokens, width))
    returned = lax.all_to_all(
        grad_slots.reshape(videos, per_slot, tokens, width),
        "dev",
        split_axis=0,
        concat_axis=0,
        tiled=True,
    ).reshape(videos * per_slot, tokens, width)
    memory_grad = gather(target, jnp.ones_like(target), returned)

    kv_terms = jnp.concatenate(
        [dot(memory_half, d_kv[0], TN), dot(memory_half, d_kv[1], TN)], axis=1
    ).astype(jnp.bfloat16)
    kv_grad = lax.psum_scatter(
        kv_terms, ("section", "dev"), scatter_dimension=0, tiled=True
    ).astype(jnp.float32)

    other = swap(partial[:, caplen:])
    merged = (
        partial[:, :caplen].astype(jnp.float32) + other.astype(jnp.float32)
    ).astype(jnp.bfloat16)
    decoded = (x + dot(merged[0], w_output)).astype(jnp.bfloat16)
    d_scaled = dot(merged[1], w_query, NT) * caption_gain
    caption_grad = grad_out.astype(jnp.float32) + inv_rms * (
        d_scaled - x * inv_rms * inv_rms * jnp.mean(d_scaled * x, axis=-1, keepdims=True)
    )
    return (
        decoded[None, None],
        caption_grad.astype(jnp.bfloat16)[None, None],
        memory_grad,
        kv_grad,
    )


def solution(mesh):
    return jax.shard_map(
        local,
        mesh=mesh,
        in_specs=(
            P(("section", "dev"), None, None),
            P(),
            P(),
            P(),
            P(),
            P(),
            P("section", "dev", None, None),
            P("section", "dev"),
            P(),
            P(),
            P(),
            P(),
            P("section", "dev", None, None),
        ),
        out_specs=(
            P("section", "dev", None, None),
            P("section", "dev", None, None),
            P(("section", "dev"), None, None),
            P(("section", "dev"), None),
        ),
        check_vma=False,
    )
```

profile of v0, /device:TPU:0, one launch (start us, length us, event | category | flops | bytes accessed | tf_op | source)
XLA Modules:
  0.0 279.2 jit_solution(11289819753831168006)
XLA Ops:
  8.4 1.6 copy-done.5
  12.7 9.8 %compress.1 = bf16[32,32,1024]{2,1,0:T(8,128)(2,1)S(1)} custom-call(s32[32]{0:T(128)S(1)} %select_reduce_fusion.1.index_ref, bf16[16,32,1024]{2,1,0:T(8,128)(2,1)S(1)} %copy-done.6, bf16[32,1024]{1,0:T(8,128)(2,1)S(1)} %copy-done.7, bf16[1024,2048]{1,0:T(8,128)(2,1)} %kv_ref.1, bf16[1024,1024]{1,0:T(8,128)(2,1)S(1)} %copy-done.5, f32[1,1024]{1,0:T(1,128)S(1)} %bitcast.77), custom_call_target="tpu_custom_call" | custom-call | flops 4294967296 | bytes 12582912 | tf_op jit(solution)/shard_map/compress/pallas_call | solution.py:74
  23.8 7.5 %all-to-all-start = ((bf16[16,2,32,1024]{3,2,1,0:T(8,128)(2,1)}), bf16[16,2,32,1024]{3,2,1,0:T(8,128)(2,1)S(1)}, u32[]{:S(2)}, u32[]{:S(2)}) async-start(bf16[16,2,32,1024]{3,2,1,0:T(8,128)(2,1)} %bitcast.72), calls=%async_computation | async-start | bytes 4194304 | tf_op jit(solution)/shard_map/all_to_all | solution.py:302
  32.3 3.9 %fusion.15 = bf16[1,128,1024]{2,1,0:T(8,128)(2,1)S(1)} fusion(bf16[1024,2048]{1,0:T(8,128)(2,1)} %param.24, bf16[1,1,128,2048]{3,2,1,0:T(8,128)(2,1)S(1)} %copy-done.13, pred[128]{0:T(512)(128)(4,1)S(1)} %iota_compare_fusion.3), kind=kOutput, calls=%fused_computation.25 | convolution fusion | flops 537264128 | bytes 4980864 | tf_op jit(solution)/shard_map/dot_general | solution.py:19
  41.8 9.7 %collective-permute-done = bf16[2,128,1024]{2,1,0:T(8,128)(2,1)} collective-permute-done((bf16[2,128,1024]{2,1,0:T(8,128)(2,1)S(1)}, bf16[2,128,1024]{2,1,0:T(8,128)(2,1)}, u32[]{:S(2)}, u32[]{:S(2)}) %collective-permute-start) | collective-permute-done | bytes 524320 | tf_op jit(solution)/shard_map/ppermute | solution.py:238
  52.8 19.6 %all-to-all-done = bf16[16,2,32,1024]{3,2,1,0:T(8,128)(2,1)S(1)} async-done(((bf16[16,2,32,1024]{3,2,1,0:T(8,128)(2,1)}), bf16[16,2,32,1024]{3,2,1,0:T(8,128)(2,1)S(1)}, u32[]{:S(2)}, u32[]{:S(2)}) %all-to-all-start) | async-done | bytes 2097184 | tf_op jit(solution)/shard_map/all_to_all | solution.py:302
  73.4 5.3 %convolution_convert_fusion.k_ref.v_ref = bf16[640,2048]{1,0:T(8,128)(2,1)S(1)} fusion(bf16[640,1024]{1,0:T(8,128)(2,1)S(1)} %bitcast.73, bf16[1024,2048]{1,0:T(8,128)(2,1)} %param.23), kind=kOutput, calls=%fused_computation.1 | convolution fusion | flops 2685665280 | bytes 8126464 | tf_op jit(solution)/shard_map/dot_general | solution.py:19
  78.7 7.2 %attention_stats.1.mine_ref = f32[8,8,256]{2,1,0:T(8,128)S(1)} custom-call(s32[1]{0:T(128)} %bitcast.2.live_ref, bf16[256,1024]{1,0:T(8,128)(2,1)S(1)} %get-tuple-element.25.q_ref, bf16[256,1024]{1,0:T(8,128)(2,1)S(1)} %get-tuple-element.24.g_ref, bf16[640,2048]{1,0:T(8,128)(2,1)S(1)} %convolution_convert_fusion.k_ref.v_ref, ...), custom_call_target="tpu_custom_call" | custom-call | tf_op jit(solution)/shard_map/attention_stats/pallas_call | solution.py:198
  86.0 1.6 collective-permute-start.1
  87.5 3.5 %collective-permute-done.1 = f32[8,8,256]{2,1,0:T(8,128)S(1)} collective-permute-done((f32[8,8,256]{2,1,0:T(8,128)S(1)}, f32[8,8,256]{2,1,0:T(8,128)S(1)}, u32[]{:S(2)}, u32[]{:S(2)}) %collective-permute-start.1) | collective-permute-done | bytes 65568 | tf_op jit(solution)/shard_map/ppermute | solution.py:238
  91.0 13.2 %attention_grads.1 = (bf16[2,256,1024]{2,1,0:T(8,128)(2,1)S(1)}, bf16[2,640,1024]{2,1,0:T(8,128)(2,1)S(1)}) custom-call(s32[1]{0:T(128)} %bitcast.2.live_ref, bf16[256,1024]{1,0:T(8,128)(2,1)S(1)} %get-tuple-element.25.q_ref, bf16[256,1024]{1,0:T(8,128)(2,1)S(1)} %get-tuple-element.24.g_ref, bf16[640,2048]{1,0:T(8,128)(2,1)S(1)} %convolution_convert_fusion.k_ref.v_ref, ...), custom_call_target="tpu_custom_call" | custom-call | tf_op jit(solution)/shard_map/attention_grads/pallas_call | solution.py:217
  104.2 1.9 convolution_convert_fusion.1
  106.1 1.9 convolution_convert_fusion.2
  108.0 2.4 pad_maximum_fusion
  110.4 6.5 %copy.25 = bf16[1024,2048]{1,0:T(8,128)(2,1)} copy(bf16[1024,2048]{0,1:T(8,128)(2,1)} %pad_maximum_fusion) | data formatting | bytes 8388608
  118.7 3.3 %fusion.2 = f32[640,1024]{1,0:T(8,128)S(1)} fusion(bf16[1024,2048]{1,0:T(8,128)(2,1)} %param.23, bf16[2,640,1024]{2,1,0:T(8,128)(2,1)S(1)} %copy-done.4), kind=kOutput, calls=%fused_computation.7 | convolution fusion | flops 1342177280 | bytes 6029312 | tf_op jit(solution)/shard_map/dot_general | solution.py:19
  122.0 1.6 add_convert_fusion
  123.6 2.3 gather.4
  125.9 10.8 %all-to-all-start.1 = ((bf16[16,2,32,1024]{3,2,1,0:T(8,128)(2,1)}), bf16[16,2,32,1024]{3,2,1,0:T(8,128)(2,1)S(1)}, u32[]{:S(2)}, u32[]{:S(2)}) async-start(bf16[16,2,32,1024]{3,2,1,0:T(8,128)(2,1)} %bitcast.24), calls=%async_computation.1 | async-start | bytes 4194304 | tf_op jit(solution)/shard_map/all_to_all | solution.py:320
  138.4 12.7 %collective-permute-done.2 = bf16[2,128,1024]{2,1,0:T(8,128)(2,1)S(1)} collective-permute-done((bf16[2,128,1024]{2,1,0:T(8,128)(2,1)S(1)}, bf16[2,128,1024]{2,1,0:T(8,128)(2,1)S(1)}, u32[]{:S(2)}, u32[]{:S(2)}) %collective-permute-start.2) | collective-permute-done | bytes 524320 | tf_op jit(solution)/shard_map/ppermute | solution.py:238
  151.3 4.0 %fusion.27 = (f32[128]{0:T(128)S(1)}, f32[128,2048]{1,0:T(8,128)S(1)}) fusion(bf16[1,1,128,2048]{3,2,1,0:T(8,128)(2,1)S(1)} %copy-done.12, f32[2048]{0:T(1024)S(1)} %copy-done.15, bf16[2048,1024]{1,0:T(8,128)(2,1)} %param.22, bf16[2,128,1024]{2,1,0:T(8,128)(2,1)S(1)} %add_convert_fusion.1), kind=kOutput, calls=%fused_computation.37 | convolution fusion | flops 537919360 | bytes 6038016 | tf_op jit(solution)/shard_map/dot_general | solution.py:19
  158.0 26.7 %all-to-all-done.1 = bf16[16,2,32,1024]{3,2,1,0:T(8,128)(2,1)S(1)} async-done(((bf16[16,2,32,1024]{3,2,1,0:T(8,128)(2,1)}), bf16[16,2,32,1024]{3,2,1,0:T(8,128)(2,1)S(1)}, u32[]{:S(2)}, u32[]{:S(2)}) %all-to-all-start.1) | async-done | bytes 2097184 | tf_op jit(solution)/shard_map/all_to_all | solution.py:320
  184.7 1.7 gather.5
  186.5 83.8 %reduce-scatter.4.cloned.1.call-done = bf16[32,2048]{1,0:T(8,128)(2,1)} async-done(((bf16[1024,2048]{1,0:T(8,128)(2,1)}), bf16[32,2048]{1,0:T(8,128)(2,1)}) %reduce-scatter.4.cloned.1.call-update) | async-done | bytes 131088
  (73 shorter events, 21.1 us)
Async XLA Ops:
  8.4 1.6 copy-start.5
  10.0 1.2 copy-start.6
  11.2 0.8 copy-start.7
  12.1 0.7 copy-start.8
  22.5 1.3 copy-start
  23.8 8.3 %copy-start.11 = (bf16[1,1,128,2048]{3,2,1,0:T(8,128)(2,1)S(1)}, bf16[1,1,128,2048]{3,2,1,0:T(8,128)(2,1)}, u32[]{:S(2)}) copy-start(bf16[1,1,128,2048]{3,2,1,0:T(8,128)(2,1)} %param.19) | copy-start | bytes 1572868
  23.8 8.5 %copy-start.13 = (bf16[1,1,128,2048]{3,2,1,0:T(8,128)(2,1)S(1)}, bf16[1,1,128,2048]{3,2,1,0:T(8,128)(2,1)}, u32[]{:S(2)}) copy-start(bf16[1,1,128,2048]{3,2,1,0:T(8,128)(2,1)} %param.25) | copy-start | bytes 1572868
  23.8 48.5 %all-to-all-start = ((bf16[16,2,32,1024]{3,2,1,0:T(8,128)(2,1)}), bf16[16,2,32,1024]{3,2,1,0:T(8,128)(2,1)S(1)}, u32[]{:S(2)}, u32[]{:S(2)}) async-start(bf16[16,2,32,1024]{3,2,1,0:T(8,128)(2,1)} %bitcast.72), calls=%async_computation | async-start | bytes 4194304 | tf_op jit(solution)/shard_map/all_to_all | solution.py:302
  31.4 238.9 %reduce-scatter.4.cloned.1.call-start = ((), (), s32[]{:S(2)}) async-start(), calls=%async_computation.3 | async-start | bytes 4325376
  32.3 3.9 %copy-start.9 = (bf16[2048,1024]{1,0:T(8,128)(2,1)S(1)}, bf16[2048,1024]{1,0:T(8,128)(2,1)}, u32[]{:S(2)}) copy-start(bf16[2048,1024]{1,0:T(8,128)(2,1)} %param.22) | copy-start | bytes 12582916
  32.3 3.9 %copy-start.15 = (f32[2048]{0:T(1024)S(1)}, f32[2048]{0:T(1024)}, u32[]{:S(2)}) copy-start(f32[2048]{0:T(1024)} %param.21) | copy-start | bytes 24580
  36.3 2.4 copy-start.16
  37.1 14.4 %collective-permute-start = (bf16[2,128,1024]{2,1,0:T(8,128)(2,1)S(1)}, bf16[2,128,1024]{2,1,0:T(8,128)(2,1)}, u32[]{:S(2)}, u32[]{:S(2)}) collective-permute-start(bf16[2,128,1024]{2,1,0:T(8,128)(2,1)S(1)} %pad_maximum_fusion.2), channel_id=1, source_target_pairs={{0,16},{16,0},{1,17},{17,1},{2,18},{18,2},{3,19},{19,3},{4,20},{20... | collective-permute-start | bytes 1572872 | tf_op jit(solution)/shard_map/ppermute | solution.py:238
  86.0 5.0 %collective-permute-start.1 = (f32[8,8,256]{2,1,0:T(8,128)S(1)}, f32[8,8,256]{2,1,0:T(8,128)S(1)}, u32[]{:S(2)}, u32[]{:S(2)}) collective-permute-start(f32[8,8,256]{2,1,0:T(8,128)S(1)} %attention_stats.1.mine_ref), channel_id=1, source_target_pairs={{0,16},{16,0},{1,17},{17,1},{2,18},{18,2},{3,19},{19,3},{4,20},{20... | collective-permute-start | bytes 196616 | tf_op jit(solution)/shard_map/ppermute | solution.py:238
  104.2 1.9 copy-start.1
  104.2 1.9 copy-start.3
  116.9 1.8 copy-start.4
  118.7 3.3 %copy-start.17 = (bf16[1024,2048]{1,0:T(8,128)(2,1)S(1)}, bf16[1024,2048]{1,0:T(8,128)(2,1)}, u32[]{:S(2)}) copy-start(bf16[1024,2048]{1,0:T(8,128)(2,1)} %param.23) | copy-start | bytes 12582916
  125.9 10.8 %copy-start.2 = (bf16[2,256,1024]{2,1,0:T(8,128)(2,1)S(1)}, bf16[2,256,1024]{2,1,0:T(8,128)(2,1)}, u32[]{:S(2)}) copy-start(bf16[2,256,1024]{2,1,0:T(8,128)(2,1)} %copy-done.1) | copy-start | bytes 3145732
  125.9 58.8 %all-to-all-start.1 = ((bf16[16,2,32,1024]{3,2,1,0:T(8,128)(2,1)}), bf16[16,2,32,1024]{3,2,1,0:T(8,128)(2,1)S(1)}, u32[]{:S(2)}, u32[]{:S(2)}) async-start(bf16[16,2,32,1024]{3,2,1,0:T(8,128)(2,1)} %bitcast.24), calls=%async_computation.1 | async-start | bytes 4194304 | tf_op jit(solution)/shard_map/all_to_all | solution.py:320
  136.7 14.6 %copy-start.12 = (bf16[1,1,128,2048]{3,2,1,0:T(8,128)(2,1)S(1)}, bf16[1,1,128,2048]{3,2,1,0:T(8,128)(2,1)}, u32[]{:S(2)}) copy-start(bf16[1,1,128,2048]{3,2,1,0:T(8,128)(2,1)} %param.19) | copy-start | bytes 1572868
  136.8 14.3 %collective-permute-start.2 = (bf16[2,128,1024]{2,1,0:T(8,128)(2,1)S(1)}, bf16[2,128,1024]{2,1,0:T(8,128)(2,1)S(1)}, u32[]{:S(2)}, u32[]{:S(2)}) collective-permute-start(bf16[2,128,1024]{2,1,0:T(8,128)(2,1)S(1)} %slice.45), channel_id=1, source_target_pairs={{0,16},{16,0},{1,17},{17,1},{2,18},{18,2},{3,19},{19,3},{4,20},{20... | collective-permute-start | bytes 1572872 | tf_op jit(solution)/shard_map/ppermute | solution.py:238
  151.3 4.0 %copy-start.10 = (bf16[1024,2048]{1,0:T(8,128)(2,1)S(1)}, bf16[1024,2048]{1,0:T(8,128)(2,1)}, u32[]{:S(2)}) copy-start(bf16[1024,2048]{1,0:T(8,128)(2,1)} %param.24) | copy-start | bytes 12582916
  155.3 1.5 copy-start.14
Sparse Core Ops, SparseCore 0:
  117.1 153.1 reduce-scatter.3
where the time goes:
time: 280 us; the launch traced here: 279 us
  waiting for transfers between devices  156 us (56%)
  Pallas kernels  35.2 us (13%)
  matrix products  24.1 us (9%)
  starting transfers between devices  23 us (8%)
  local copies, waits for them, and re-layouts  17.3 us (6%)
  between operations  15.7 us (6%)
  other arithmetic  7.89 us (3%)
    unnamed x2, waiting for transfers between devices  83.8 us
    all_to_all x1, waiting for transfers between devices, local(): lax.all_to_all(grad_slots.reshape(videos, per_slot, tokens, width), 'dev'...  26.7 us
    ppermute x3, waiting for transfers between devices, swap(): return lax.ppermute(x, 'section', [(0, 1), (1, 0)])  25.9 us
    dot_general x9, matrix products, dot(): return lax.dot_general(a, b, dims, preferred_element_type=jnp.float32)  24.1 us
    all_to_all x1, waiting for transfers between devices, local(): lax.all_to_all(packed.reshape(videos, per_slot, tokens, width), 'dev', sp...  19.6 us
    unnamed x39, local copies, waits for them, and re-layouts  15.2 us
    pallas_call x1, Pallas kernels, attention_grads(): pl.pallas_call(grads_kernel, grid_spec=pltpu.PrefetchScalarGridSpec(num_s...  13.2 us
    all_to_all x1, starting transfers between devices, local(): lax.all_to_all(grad_slots.reshape(videos, per_slot, tokens, width), 'dev'...  10.8 us
  transfers between devices with their start and end apart: 6, of which 6 were waited for; matrix products, arithmetic and copies ran while one was open for 8% of the time, Pallas kernels for 1%

commit v1 on v0

--- a/solution.py
+++ b/solution.py
@@ -1,3 +1,5 @@
+import functools
+
 import jax
 import jax.numpy as jnp
 from jax import lax
@@ -12,7 +14,6 @@
 NT = (((1,), (1,)), ((), ()))
 TN = (((0,), (0,)), ((), ()))
 LANES = 128
-VMEM = 60 * 1024 * 1024
 
 
 def dot(a, b, dims=(((1,), (0,)), ((), ()))):
@@ -234,6 +235,102 @@
     )(live, q, g, kv, kv, mine, peer)
 
 
+def halving_orders(bits):
+    middle = list(range(bits - 1, 0, -1))
+    return [bits, 0] + middle, [bits] + middle[:1] + [0] + middle[1:]
+
+
+def reduce_kernel(bits, a_ref, b_ref, out_ref, *scratch):
+    stages = bits + 1
+    got, held = scratch[: 2 * stages], scratch[2 * stages : 4 * stages - 2]
+    send_sem, recv_sem = scratch[-2:]
+    section, dev = lax.axis_index("section"), lax.axis_index("dev")
+    mine = [section] + [lax.rem(dev // 2 ** (bits - t), 2) for t in range(1, bits + 1)]
+    peers = [(1 - section, dev)] + [
+        (section, dev + (1 - 2 * mine[t]) * 2 ** (bits - t)) for t in range(1, bits + 1)
+    ]
+    barrier = pltpu.get_barrier_semaphore()
+    for peer in peers:
+        pl.semaphore_signal(barrier, inc=1, device_id=peer, device_id_type=pl.DeviceIdType.MESH)
+    pl.semaphore_wait(barrier, stages)
+
+    orders = halving_orders(bits)
+    width = a_ref.shape[-1]
+
+    def source(chain, stage):
+        return (a_ref, b_ref)[chain] if stage == 0 else held[chain * (stages - 1) + stage - 1]
+
+    def place(chain, stage):
+        done = orders[chain][:stage]
+        return sum(1 for t in range(orders[chain][stage]) if t not in done)
+
+    def copy(chain, stage):
+        at = (slice(None),) * place(chain, stage)
+        t = orders[chain][stage]
+        return pltpu.make_async_remote_copy(
+            src_ref=source(chain, stage).at[at + (1 - mine[t],)],
+            dst_ref=got[chain * stages + stage],
+            send_sem=send_sem.at[chain * stages + stage],
+            recv_sem=recv_sem.at[chain * stages + stage],
+            device_id=peers[t],
+            device_id_type=pl.DeviceIdType.MESH,
+        )
+
+    copies = {(c, 0): copy(c, 0) for c in range(2)}
+    for c in range(2):
+        copies[c, 0].start()
+    for stage in range(stages):
+        for c in range(2):
+            copies[c, stage].wait_recv()
+            left = stages - 1 - stage
+            at, bit = place(c, stage), mine[orders[c][stage]]
+            src, other = source(c, stage), got[c * stages + stage]
+
+            def add(i, carry):
+                index = tuple(lax.rem(i // 2 ** (left - 1 - n), 2) for n in range(left))
+                total = src[index[:at] + (bit,) + index[at:]].astype(jnp.float32)
+                total = total + other[index].astype(jnp.float32)
+                if left:
+                    held[c * (stages - 1) + stage][index] = total.astype(jnp.bfloat16)
+                else:
+                    out_ref[:, c * width : (c + 1) * width] = total
+                return carry
+
+            if left:
+                lax.fori_loop(0, 2**left, add, 0)
+                copies[c, stage + 1] = copy(c, stage + 1)
+                copies[c, stage + 1].start()
+            else:
+                add(0, 0)
+    for made in copies.values():
+        made.wait_send()
+
+
+def reduce_rows(a, b):
+    n_section, n_dev = lax.axis_size("section"), lax.axis_size("dev")
+    bits = n_dev.bit_length() - 1
+    rows = a.shape[0] // (n_section * n_dev)
+    width = a.shape[1]
+    stages = bits + 1
+    block = lambda n: pltpu.VMEM((2,) * n + (rows, width), jnp.bfloat16)
+    return pl.pallas_call(
+        functools.partial(reduce_kernel, bits),
+        out_shape=jax.ShapeDtypeStruct((rows, 2 * width), jnp.float32),
+        in_specs=[pl.BlockSpec(memory_space=pltpu.VMEM)] * 2,
+        out_specs=pl.BlockSpec(memory_space=pltpu.VMEM),
+        scratch_shapes=[block(stages - 1 - s) for _ in range(2) for s in range(stages)]
+        + [block(stages - 1 - s) for _ in range(2) for s in range(stages - 1)]
+        + [pltpu.SemaphoreType.DMA((2 * stages,)), pltpu.SemaphoreType.DMA((2 * stages,))],
+        compiler_params=pltpu.CompilerParams(
+            collective_id=0, has_side_effects=True, vmem_limit_bytes=32 * 1024 * 1024
+        ),
+        cost_estimate=pl.CostEstimate(
+            flops=0, bytes_accessed=64 * 1024 * 1024, transcendentals=0
+        ),
+        name="reduce_rows",
+    )(*(v.reshape((2,) * stages + (rows, width)) for v in (a, b)))
+
+
 def swap(x):
     return lax.ppermute(x, "section", [(0, 1), (1, 0)])
 
@@ -326,12 +423,9 @@
     ).reshape(videos * per_slot, tokens, width)
     memory_grad = gather(target, jnp.ones_like(target), returned)
 
-    kv_terms = jnp.concatenate(
-        [dot(memory_half, d_kv[0], TN), dot(memory_half, d_kv[1], TN)], axis=1
-    ).astype(jnp.bfloat16)
-    kv_grad = lax.psum_scatter(
-        kv_terms, ("section", "dev"), scatter_dimension=0, tiled=True
-    ).astype(jnp.float32)
+    terms = [dot(memory_half, d_kv[n], TN).astype(jnp.bfloat16) for n in range(2)]
+    *terms, _ = lax.optimization_barrier((*terms, grad_slots))
+    kv_grad = reduce_rows(*terms)
 
     other = swap(partial[:, caplen:])
     merged = (

time: 280 us -> 184 us (0.66)
  waiting for transfers between devices: 156 us -> 32.1 us
  Pallas kernels: 35.2 us -> 88.3 us
  between operations: 15.7 us -> 2.33 us
  local copies, waits for them, and re-layouts: 17.3 us -> 10.4 us
    unnamed x2 -> x0, waiting for transfers between devices: 83.8 us -> none
    pallas_call x0 -> x1, Pallas kernels: none -> 53.3 us  [reduce_rows(): pl.pallas_call(functools.partial(reduce_kernel, bits), out_shape=jax.Shap...]
    all_to_all x1, waiting for transfers between devices: 26.7 us -> 0.01 us  [local(): lax.all_to_all(grad_slots.reshape(videos, per_slot, tokens, width), 'dev'...]
    ppermute x3, waiting for transfers between devices: 25.9 us -> 12.4 us  [swap(): return lax.ppermute(x, 'section', [(0, 1), (1, 0)])]
    unnamed x39 -> x43, local copies, waits for them, and re-layouts: 15.2 us -> 7.24 us
  transfers between devices with their start and end apart: 6 -> 5, of which waited for: 6 -> 3; matrix products, arithmetic and copies ran while one was open for 8% -> 11% of each run, Pallas kernels for 1% -> 29%
where the time goes in v1:
time: 184 us; the launch traced here: 183 us
  Pallas kernels  88.3 us (48%)
  waiting for transfers between devices  32.1 us (17%)
  starting transfers between devices  23 us (12%)
  matrix products  21.7 us (12%)
  local copies, waits for them, and re-layouts  10.4 us (6%)
  other arithmetic  5.34 us (3%)
  between operations  2.33 us (1%)
    pallas_call x1, Pallas kernels, reduce_rows(): pl.pallas_call(functools.partial(reduce_kernel, bits), out_shape=jax.Shap...  53.3 us
    dot_general x9, matrix products, dot(): return lax.dot_general(a, b, dims, preferred_element_type=jnp.float32)  21.7 us
    all_to_all x1, waiting for transfers between devices, local(): lax.all_to_all(packed.reshape(videos, per_slot, tokens, width), 'dev', sp...  19.6 us
    pallas_call x1, Pallas kernels, attention_grads(): pl.pallas_call(grads_kernel, grid_spec=pltpu.PrefetchScalarGridSpec(num_s...  13.2 us
    ppermute x3, waiting for transfers between devices, swap(): return lax.ppermute(x, 'section', [(0, 1), (1, 0)])  12.4 us
    all_to_all x1, starting transfers between devices, local(): lax.all_to_all(grad_slots.reshape(videos, per_slot, tokens, width), 'dev'...  10.8 us
    pallas_call x1, Pallas kernels, compress(): pl.pallas_call(compress_kernel, grid_spec=pltpu.PrefetchScalarGridSpec(nu...  9.75 us
    all_to_all x1, starting transfers between devices, local(): lax.all_to_all(packed.reshape(videos, per_slot, tokens, width), 'dev', sp...  7.55 us
  transfers between devices with their start and end apart: 5, of which 3 were waited for; matrix products, arithmetic and copies ran while one was open for 11% of the time, Pallas kernels for 29%

profile of v1, /device:TPU:0, one launch (start us, length us, event | category | flops | bytes accessed | tf_op | source)
XLA Modules:
  0.0 183.1 jit_solution(6110258082011146021)
XLA Ops:
  1.9 1.6 copy-done.7
  6.2 9.8 %compress.1 = bf16[32,32,1024]{2,1,0:T(8,128)(2,1)S(1)} custom-call(s32[32]{0:T(128)S(1)} %select_reduce_fusion.1.index_ref, bf16[16,32,1024]{2,1,0:T(8,128)(2,1)S(1)} %copy-done.8, bf16[32,1024]{1,0:T(8,128)(2,1)S(1)} %copy-done.9, bf16[1024,2048]{1,0:T(8,128)(2,1)} %kv_ref.1, bf16[1024,1024]{1,0:T(8,128)(2,1)S(1)} %copy-done.7, f32[1,1024]{1,0:T(1,128)S(1)} %bitcast.80), custom_call_target="tpu_custom_call" | custom-call | flops 4294967296 | bytes 12582912 | tf_op jit(solution)/shard_map/compress/pallas_call | solution.py:75
  16.0 1.3 copy-done
  17.3 7.5 %all-to-all-start = ((bf16[16,2,32,1024]{3,2,1,0:T(8,128)(2,1)}), bf16[16,2,32,1024]{3,2,1,0:T(8,128)(2,1)S(1)}, u32[]{:S(2)}, u32[]{:S(2)}) async-start(bf16[16,2,32,1024]{3,2,1,0:T(8,128)(2,1)} %bitcast.73), calls=%async_computation | async-start | bytes 4194304 | tf_op jit(solution)/shard_map/all_to_all | solution.py:399
  25.8 3.9 %fusion.15 = bf16[1,128,1024]{2,1,0:T(8,128)(2,1)S(1)} fusion(bf16[1024,2048]{1,0:T(8,128)(2,1)} %param.24, bf16[1,1,128,2048]{3,2,1,0:T(8,128)(2,1)S(1)} %copy-done.16, pred[128]{0:T(512)(128)(4,1)S(1)} %iota_compare_fusion.3), kind=kOutput, calls=%fused_computation.24 | convolution fusion | flops 537264128 | bytes 4980864 | tf_op jit(solution)/shard_map/dot_general | solution.py:20
  30.5 1.6 collective-permute-start
  35.9 9.0 %collective-permute-done = bf16[2,128,1024]{2,1,0:T(8,128)(2,1)} collective-permute-done((bf16[2,128,1024]{2,1,0:T(8,128)(2,1)S(1)}, bf16[2,128,1024]{2,1,0:T(8,128)(2,1)}, u32[]{:S(2)}, u32[]{:S(2)}) %collective-permute-start) | collective-permute-done | bytes 524320 | tf_op jit(solution)/shard_map/ppermute | solution.py:335
  46.2 19.6 %all-to-all-done = bf16[16,2,32,1024]{3,2,1,0:T(8,128)(2,1)S(1)} async-done(((bf16[16,2,32,1024]{3,2,1,0:T(8,128)(2,1)}), bf16[16,2,32,1024]{3,2,1,0:T(8,128)(2,1)S(1)}, u32[]{:S(2)}, u32[]{:S(2)}) %all-to-all-start) | async-done | bytes 2097184 | tf_op jit(solution)/shard_map/all_to_all | solution.py:399
  66.7 5.8 %convolution_convert_fusion.k_ref.v_ref = bf16[640,2048]{1,0:T(8,128)(2,1)S(1)} fusion(bf16[640,1024]{1,0:T(8,128)(2,1)S(1)} %bitcast.76, bf16[1024,2048]{1,0:T(8,128)(2,1)} %param.23), kind=kOutput, calls=%fused_computation | convolution fusion | flops 2685665280 | bytes 8126464 | tf_op jit(solution)/shard_map/dot_general | solution.py:20
  72.4 7.2 %attention_stats.1.mine_ref = f32[8,8,256]{2,1,0:T(8,128)S(1)} custom-call(s32[1]{0:T(128)} %bitcast.2.live_ref, bf16[256,1024]{1,0:T(8,128)(2,1)S(1)} %get-tuple-element.13.q_ref, bf16[256,1024]{1,0:T(8,128)(2,1)S(1)} %get-tuple-element.12.g_ref, bf16[640,2048]{1,0:T(8,128)(2,1)S(1)} %convolution_convert_fusion.k_ref.v_ref, ...), custom_call_target="tpu_custom_call" | custom-call | tf_op jit(solution)/shard_map/attention_stats/pallas_call | solution.py:199
  79.7 1.6 collective-permute-start.1
  81.3 3.4 %collective-permute-done.1 = f32[8,8,256]{2,1,0:T(8,128)S(1)} collective-permute-done((f32[8,8,256]{2,1,0:T(8,128)S(1)}, f32[8,8,256]{2,1,0:T(8,128)S(1)}, u32[]{:S(2)}, u32[]{:S(2)}) %collective-permute-start.1) | collective-permute-done | bytes 65568 | tf_op jit(solution)/shard_map/ppermute | solution.py:335
  84.7 13.2 %attention_grads.1 = (bf16[2,256,1024]{2,1,0:T(8,128)(2,1)S(1)}, bf16[2,640,1024]{2,1,0:T(8,128)(2,1)S(1)}) custom-call(s32[1]{0:T(128)} %bitcast.2.live_ref, bf16[256,1024]{1,0:T(8,128)(2,1)S(1)} %get-tuple-element.13.q_ref, bf16[256,1024]{1,0:T(8,128)(2,1)S(1)} %get-tuple-element.12.g_ref, bf16[640,2048]{1,0:T(8,128)(2,1)S(1)} %convolution_convert_fusion.k_ref.v_ref, ...), custom_call_target="tpu_custom_call" | custom-call | tf_op jit(solution)/shard_map/attention_grads/pallas_call | solution.py:218
  98.0 1.6 fusion.2
  99.8 1.6 add_convert_fusion
  101.4 2.3 %gather.4 = bf16[32,32,1024]{2,1,0:T(8,128)(2,1)} custom-call(s32[32]{0:T(128)S(1)} %select_reduce_fusion.index_ref, s32[32]{0:T(128)S(1)} %broadcast_in_dim.66.live_ref, bf16[20,32,1024]{2,1,0:T(8,128)(2,1)S(1)} %bitcast.79), custom_call_target="tpu_custom_call" | custom-call | tf_op jit(solution)/shard_map/gather/pallas_call | solution.py:117
  103.7 10.8 %all-to-all-start.1 = ((bf16[16,2,32,1024]{3,2,1,0:T(8,128)(2,1)}), bf16[16,2,32,1024]{3,2,1,0:T(8,128)(2,1)S(1)}, u32[]{:S(2)}, u32[]{:S(2)}) async-start(bf16[16,2,32,1024]{3,2,1,0:T(8,128)(2,1)} %bitcast.24), calls=%async_computation.1 | async-start | bytes 4194304 | tf_op jit(solution)/shard_map/all_to_all | solution.py:417
  115.5 1.6 collective-permute-start.2
  117.1 3.2 %convolution_convert_fusion.1 = bf16[1024,1024]{1,0:T(8,128)(2,1)S(1)} fusion(bf16[640,1024]{1,0:T(8,128)(2,1)S(1)} %bitcast.77, bf16[2,640,1024]{2,1,0:T(8,128)(2,1)} %copy-done.5), kind=kOutput, calls=%fused_computation.10 | convolution fusion | flops 1343225856 | bytes 4718592 | tf_op jit(solution)/shard_map/dot_general | solution.py:20
  120.3 1.8 %convolution_convert_fusion.2 = bf16[1024,1024]{1,0:T(8,128)(2,1)S(1)} fusion(bf16[640,1024]{1,0:T(8,128)(2,1)S(1)} %bitcast.78, bf16[2,640,1024]{2,1,0:T(8,128)(2,1)S(1)} %copy-done.6), kind=kOutput, calls=%fused_computation.11 | convolution fusion | flops 1343225856 | bytes 4718592 | tf_op jit(solution)/shard_map/dot_general | solution.py:20
  122.2 53.3 %reduce_rows.1 = f32[32,2048]{1,0:T(8,128)S(1)} custom-call(bf16[2,2,2,2,2,32,1024]{6,5,4,3,2,1,0:T(8,128)(2,1)S(1)} %bitcast.75, bf16[2,2,2,2,2,32,1024]{6,5,4,3,2,1,0:T(8,128)(2,1)S(1)} %bitcast.74), custom_call_target="tpu_custom_call" | custom-call | bytes 67108864 | tf_op jit(solution)/shard_map/reduce_rows/pallas_call | solution.py:316
  175.7 1.6 fusion.27
  177.9 1.6 fusion.1
  180.7 1.7 gather.5
  (74 shorter events, 14.4 us)
Async XLA Ops:
  1.9 1.6 copy-start.7
  3.5 1.2 copy-start.8
  16.0 1.3 copy-start
  17.3 8.2 %copy-start.14 = (bf16[1,1,128,2048]{3,2,1,0:T(8,128)(2,1)S(1)}, bf16[1,1,128,2048]{3,2,1,0:T(8,128)(2,1)}, u32[]{:S(2)}) copy-start(bf16[1,1,128,2048]{3,2,1,0:T(8,128)(2,1)} %param.19) | copy-start | bytes 1572868
  17.3 8.4 %copy-start.16 = (bf16[1,1,128,2048]{3,2,1,0:T(8,128)(2,1)S(1)}, bf16[1,1,128,2048]{3,2,1,0:T(8,128)(2,1)}, u32[]{:S(2)}) copy-start(bf16[1,1,128,2048]{3,2,1,0:T(8,128)(2,1)} %param.25) | copy-start | bytes 1572868
  17.3 48.5 %all-to-all-start = ((bf16[16,2,32,1024]{3,2,1,0:T(8,128)(2,1)}), bf16[16,2,32,1024]{3,2,1,0:T(8,128)(2,1)S(1)}, u32[]{:S(2)}, u32[]{:S(2)}) async-start(bf16[16,2,32,1024]{3,2,1,0:T(8,128)(2,1)} %bitcast.73), calls=%async_computation | async-start | bytes 4194304 | tf_op jit(solution)/shard_map/all_to_all | solution.py:399
  25.7 3.9 %copy-start.11 = (bf16[2048,1024]{1,0:T(8,128)(2,1)S(1)}, bf16[2048,1024]{1,0:T(8,128)(2,1)}, u32[]{:S(2)}) copy-start(bf16[2048,1024]{1,0:T(8,128)(2,1)} %param.22) | copy-start | bytes 12582916
  25.7 3.9 %copy-start.18 = (f32[2048]{0:T(1024)S(1)}, f32[2048]{0:T(1024)}, u32[]{:S(2)}) copy-start(f32[2048]{0:T(1024)} %param.21) | copy-start | bytes 24580
  29.6 2.4 %copy-start.19 = (s32[2,16]{1,0:T(2,128)S(1)}, s32[2,16]{1,0:T(2,128)}, u32[]{:S(2)}) copy-start(s32[2,16]{1,0:T(2,128)} %param.14) | copy-start | bytes 388
  30.5 14.4 %collective-permute-start = (bf16[2,128,1024]{2,1,0:T(8,128)(2,1)S(1)}, bf16[2,128,1024]{2,1,0:T(8,128)(2,1)}, u32[]{:S(2)}, u32[]{:S(2)}) collective-permute-start(bf16[2,128,1024]{2,1,0:T(8,128)(2,1)S(1)} %pad_maximum_fusion.1), channel_id=1, source_target_pairs={{0,16},{16,0},{1,17},{17,1},{2,18},{18,2},{3,19},{19,3},{4,20},{20... | collective-permute-start | bytes 1572872 | tf_op jit(solution)/shard_map/ppermute | solution.py:335
  66.7 5.8 %copy-start.1 = (bf16[20,32,1024]{2,1,0:T(8,128)(2,1)}, bf16[20,32,1024]{2,1,0:T(8,128)(2,1)S(1)}, u32[]{:S(2)}) copy-start(bf16[20,32,1024]{2,1,0:T(8,128)(2,1)S(1)} %gather.3) | copy-start | bytes 3932164
  79.7 5.0 %collective-permute-start.1 = (f32[8,8,256]{2,1,0:T(8,128)S(1)}, f32[8,8,256]{2,1,0:T(8,128)S(1)}, u32[]{:S(2)}, u32[]{:S(2)}) collective-permute-start(f32[8,8,256]{2,1,0:T(8,128)S(1)} %attention_stats.1.mine_ref), channel_id=1, source_target_pairs={{0,16},{16,0},{1,17},{17,1},{2,18},{18,2},{3,19},{19,3},{4,20},{20... | collective-permute-start | bytes 196616 | tf_op jit(solution)/shard_map/ppermute | solution.py:335
  84.7 13.2 %copy-start.20 = (bf16[1024,2048]{1,0:T(8,128)(2,1)S(1)}, bf16[1024,2048]{1,0:T(8,128)(2,1)}, u32[]{:S(2)}) copy-start(bf16[1024,2048]{1,0:T(8,128)(2,1)} %param.23) | copy-start | bytes 12582916
  97.9 1.6 copy-start.3
  97.9 1.9 %copy-start.5 = (bf16[2,640,1024]{2,1,0:T(8,128)(2,1)}, bf16[2,640,1024]{2,1,0:T(8,128)(2,1)S(1)}, u32[]{:S(2)}) copy-start(bf16[2,640,1024]{2,1,0:T(8,128)(2,1)S(1)} %get-tuple-element.9) | copy-start | bytes 7864324
  103.7 13.4 %copy-start.2 = (bf16[20,32,1024]{2,1,0:T(8,128)(2,1)S(1)}, bf16[20,32,1024]{2,1,0:T(8,128)(2,1)}, u32[]{:S(2)}) copy-start(bf16[20,32,1024]{2,1,0:T(8,128)(2,1)} %copy-done.1) | copy-start | bytes 3932164
  103.7 77.0 %all-to-all-start.1 = ((bf16[16,2,32,1024]{3,2,1,0:T(8,128)(2,1)}), bf16[16,2,32,1024]{3,2,1,0:T(8,128)(2,1)S(1)}, u32[]{:S(2)}, u32[]{:S(2)}) async-start(bf16[16,2,32,1024]{3,2,1,0:T(8,128)(2,1)} %bitcast.24), calls=%async_computation.1 | async-start | bytes 4194304 | tf_op jit(solution)/shard_map/all_to_all | solution.py:417
  115.5 4.8 %copy-start.6 = (bf16[2,640,1024]{2,1,0:T(8,128)(2,1)S(1)}, bf16[2,640,1024]{2,1,0:T(8,128)(2,1)}, u32[]{:S(2)}) copy-start(bf16[2,640,1024]{2,1,0:T(8,128)(2,1)} %copy-done.5) | copy-start | bytes 7864324
  115.5 59.9 %collective-permute-start.2 = (bf16[2,128,1024]{2,1,0:T(8,128)(2,1)S(1)}, bf16[2,128,1024]{2,1,0:T(8,128)(2,1)S(1)}, u32[]{:S(2)}, u32[]{:S(2)}) collective-permute-start(bf16[2,128,1024]{2,1,0:T(8,128)(2,1)S(1)} %slice.45), channel_id=1, source_target_pairs={{0,16},{16,0},{1,17},{17,1},{2,18},{18,2},{3,19},{19,3},{4,20},{20... | collective-permute-start | bytes 1572872 | tf_op jit(solution)/shard_map/ppermute | solution.py:335
  122.2 53.3 %copy-start.4 = (bf16[2,256,1024]{2,1,0:T(8,128)(2,1)S(1)}, bf16[2,256,1024]{2,1,0:T(8,128)(2,1)}, u32[]{:S(2)}) copy-start(bf16[2,256,1024]{2,1,0:T(8,128)(2,1)} %copy-done.3) | copy-start | bytes 3145732
  122.2 53.5 %copy-start.12 = (bf16[2048,1024]{1,0:T(8,128)(2,1)S(1)}, bf16[2048,1024]{1,0:T(8,128)(2,1)}, u32[]{:S(2)}) copy-start(bf16[2048,1024]{1,0:T(8,128)(2,1)} %param.22) | copy-start | bytes 12582916
  122.2 53.5 %copy-start.15 = (bf16[1,1,128,2048]{3,2,1,0:T(8,128)(2,1)S(1)}, bf16[1,1,128,2048]{3,2,1,0:T(8,128)(2,1)}, u32[]{:S(2)}) copy-start(bf16[1,1,128,2048]{3,2,1,0:T(8,128)(2,1)} %param.19) | copy-start | bytes 1572868
  175.7 2.2 %copy-start.13 = (bf16[1024,2048]{1,0:T(8,128)(2,1)S(1)}, bf16[1024,2048]{1,0:T(8,128)(2,1)}, u32[]{:S(2)}) copy-start(bf16[1024,2048]{1,0:T(8,128)(2,1)} %param.24) | copy-start | bytes 12582916
  177.9 1.6 copy-start.17
  (2 other events, 1.5 us)

commit v2 on v1

--- a/solution.py
+++ b/solution.py
@@ -240,25 +240,117 @@
     return [bits, 0] + middle, [bits] + middle[:1] + [0] + middle[1:]
 
 
-def reduce_kernel(bits, a_ref, b_ref, out_ref, *scratch):
+def tail_kernel(
+    bits,
+    return_ref,
+    target_ref,
+    half_ref,
+    d_kv_ref,
+    memory_kv_ref,
+    part_ref,
+    x_ref,
+    grad_out_ref,
+    gain_ref,
+    w_query_ref,
+    w_output_ref,
+    kv_grad_ref,
+    memory_grad_ref,
+    decoded_ref,
+    caption_grad_ref,
+    *scratch,
+):
+    mesh_ids = pl.DeviceIdType.MESH
     stages = bits + 1
+    n_dev = 2**bits
     got, held = scratch[: 2 * stages], scratch[2 * stages : 4 * stages - 2]
-    send_sem, recv_sem = scratch[-2:]
+    terms = scratch[4 * stages - 2 : 4 * stages]
+    (d_mem, slots, returned, other_part, w_query_s, w_output_s, send_sem, recv_sem,
+     slot_send, slot_recv, part_sem, load_sem) = scratch[4 * stages :]
     section, dev = lax.axis_index("section"), lax.axis_index("dev")
     mine = [section] + [lax.rem(dev // 2 ** (bits - t), 2) for t in range(1, bits + 1)]
     peers = [(1 - section, dev)] + [
         (section, dev + (1 - 2 * mine[t]) * 2 ** (bits - t)) for t in range(1, bits + 1)
     ]
+    loads = [
+        pltpu.make_async_copy(w_query_ref, w_query_s, load_sem.at[0]),
+        pltpu.make_async_copy(w_output_ref, w_output_s, load_sem.at[1]),
+    ]
+    for load in loads:
+        load.start()
     barrier = pltpu.get_barrier_semaphore()
-    for peer in peers:
-        pl.semaphore_signal(barrier, inc=1, device_id=peer, device_id_type=pl.DeviceIdType.MESH)
-    pl.semaphore_wait(barrier, stages)
+    pl.semaphore_signal(barrier, inc=1, device_id=peers[0], device_id_type=mesh_ids)
+
+    def greet(k, carry):
+        peer = (section, lax.rem(dev + k, n_dev))
+        pl.semaphore_signal(barrier, inc=1, device_id=peer, device_id_type=mesh_ids)
+        return carry
+
+    lax.fori_loop(1, n_dev, greet, 0)
+
+    width = half_ref.shape[1]
+    inner = d_kv_ref.shape[2]
+    chunk = width // 4
+
+    def memory_columns(j, carry):
+        at = pl.ds(pl.multiple_of(j * chunk, chunk), chunk)
+        value = dot(d_kv_ref[0], memory_kv_ref[at, :inner], NT)
+        value = value + dot(d_kv_ref[1], memory_kv_ref[at, inner:], NT)
+        d_mem[:, :, at] = value.astype(jnp.bfloat16).reshape(d_mem.shape[:2] + (chunk,))
+        return carry
+
+    lax.fori_loop(0, 4, memory_columns, 0)
+    per_slot = slots.shape[1]
+
+    def pack(i, carry):
+        slots[i // per_slot, lax.rem(i, per_slot)] = d_mem[return_ref[i]]
+        return carry
+
+    lax.fori_loop(0, n_dev * per_slot, pack, 0)
+    pl.semaphore_wait(barrier, n_dev)
+
+    def slot_copy(k):
+        to = lax.rem(dev + k, n_dev)
+        return pltpu.make_async_remote_copy(
+            src_ref=slots.at[to],
+            dst_ref=returned.at[dev],
+            send_sem=slot_send.at[k],
+            recv_sem=slot_recv.at[k],
+            device_id=(section, to),
+            device_id_type=mesh_ids,
+        )
+
+    caplen = x_ref.shape[0]
+    part_copy = pltpu.make_async_remote_copy(
+        src_ref=part_ref.at[:, pl.ds(caplen, caplen)],
+        dst_ref=other_part,
+        send_sem=part_sem.at[0],
+        recv_sem=part_sem.at[1],
+        device_id=peers[0],
+        device_id_type=mesh_ids,
+    )
+    part_copy.start()
+
+    def send_slot(i, carry):
+        slot_copy(lax.rem(i + n_dev // 2 - 1, n_dev - 1) + 1).start()
+        return carry
+
+    lax.fori_loop(0, n_dev - 1, send_slot, 0)
+    returned[dev] = slots[dev]
+
+    for c in range(2):
+
+        def term_rows(j, carry):
+            at = pl.ds(pl.multiple_of(j * chunk, chunk), chunk)
+            value = dot(half_ref[:, at], d_kv_ref[c], TN).astype(jnp.bfloat16)
+            terms[c][j // 2, lax.rem(j, 2)] = value.reshape(terms[c].shape[2:])
+            return carry
+
+        lax.fori_loop(0, 4, term_rows, 0)
 
     orders = halving_orders(bits)
-    width = a_ref.shape[-1]
 
     def source(chain, stage):
-        return (a_ref, b_ref)[chain] if stage == 0 else held[chain * (stages - 1) + stage - 1]
+        return terms[chain] if stage == 0 else held[chain * (stages - 1) + stage - 1]
 
     def place(chain, stage):
         done = orders[chain][:stage]
@@ -273,7 +365,7 @@
             send_sem=send_sem.at[chain * stages + stage],
             recv_sem=recv_sem.at[chain * stages + stage],
             device_id=peers[t],
-            device_id_type=pl.DeviceIdType.MESH,
+            device_id_type=mesh_ids,
         )
 
     copies = {(c, 0): copy(c, 0) for c in range(2)}
@@ -293,7 +385,7 @@
                 if left:
                     held[c * (stages - 1) + stage][index] = total.astype(jnp.bfloat16)
                 else:
-                    out_ref[:, c * width : (c + 1) * width] = total
+                    kv_grad_ref[:, c * inner : (c + 1) * inner] = total
                 return carry
 
             if left:
@@ -302,33 +394,97 @@
                 copies[c, stage + 1].start()
             else:
                 add(0, 0)
+        if stage == 0:
+            part_copy.wait_recv()
+            for load in loads:
+                load.wait()
+            merged = [
+                (
+                    part_ref[n, :caplen, :].astype(jnp.float32) + other_part[n].astype(jnp.float32)
+                ).astype(jnp.bfloat16)
+                for n in range(2)
+            ]
+            x = x_ref[...].astype(jnp.float32)
+            decoded_ref[...] = (x + dot(merged[0], w_output_s[...])).astype(jnp.bfloat16)
+            inv_rms = lax.rsqrt(jnp.mean(x * x, axis=-1, keepdims=True) + EPSILON)
+            d_scaled = dot(merged[1], w_query_s[...], NT) * gain_ref[...]
+            mean = jnp.mean(d_scaled * x, axis=-1, keepdims=True)
+            caption_grad_ref[...] = (
+                grad_out_ref[...].astype(jnp.float32)
+                + inv_rms * (d_scaled - x * inv_rms * inv_rms * mean)
+            ).astype(jnp.bfloat16)
+
+    def arrive(k, carry):
+        slot_copy(k).wait_recv()
+        return carry
+
+    lax.fori_loop(1, n_dev, arrive, 0)
+
+    def unpack(j, carry):
+        memory_grad_ref[j] = returned[target_ref[j] // per_slot, lax.rem(target_ref[j], per_slot)]
+        return carry
+
+    lax.fori_loop(0, memory_grad_ref.shape[0], unpack, 0)
+
+    def sent(k, carry):
+        slot_copy(k).wait_send()
+        return carry
+
+    lax.fori_loop(1, n_dev, sent, 0)
+    part_copy.wait_send()
     for made in copies.values():
         made.wait_send()
 
 
-def reduce_rows(a, b):
+def tail(return_index, target, half, d_kv, memory_kv, part, x, grad_out, gain, w_query, w_output):
     n_section, n_dev = lax.axis_size("section"), lax.axis_size("dev")
     bits = n_dev.bit_length() - 1
-    rows = a.shape[0] // (n_section * n_dev)
-    width = a.shape[1]
     stages = bits + 1
-    block = lambda n: pltpu.VMEM((2,) * n + (rows, width), jnp.bfloat16)
+    width, inner = half.shape[1], d_kv.shape[2]
+    rows = width // (n_section * n_dev)
+    caplen, model = x.shape
+    slots = (n_dev, return_index.shape[0] // n_dev, half.shape[0] // MOST_WIN, width)
+    bf16 = jnp.bfloat16
+    block = lambda n: pltpu.VMEM((2,) * n + (rows, inner), bf16)
+    vmem = pl.BlockSpec(memory_space=pltpu.VMEM)
+    smem = pl.BlockSpec(memory_space=pltpu.SMEM)
+    far = pl.BlockSpec(memory_space=pl.ANY)
+    dma = pltpu.SemaphoreType.DMA
     return pl.pallas_call(
-        functools.partial(reduce_kernel, bits),
-        out_shape=jax.ShapeDtypeStruct((rows, 2 * width), jnp.float32),
-        in_specs=[pl.BlockSpec(memory_space=pltpu.VMEM)] * 2,
-        out_specs=pl.BlockSpec(memory_space=pltpu.VMEM),
+        functools.partial(tail_kernel, bits),
+        out_shape=[
+            jax.ShapeDtypeStruct((rows, 2 * inner), jnp.float32),
+            jax.ShapeDtypeStruct((target.shape[0],) + slots[2:], bf16),
+            jax.ShapeDtypeStruct((caplen, model), bf16),
+            jax.ShapeDtypeStruct((caplen, model), bf16),
+        ],
+        in_specs=[smem] * 2 + [vmem] * 7 + [far] * 2,
+        out_specs=[vmem] * 4,
         scratch_shapes=[block(stages - 1 - s) for _ in range(2) for s in range(stages)]
         + [block(stages - 1 - s) for _ in range(2) for s in range(stages - 1)]
-        + [pltpu.SemaphoreType.DMA((2 * stages,)), pltpu.SemaphoreType.DMA((2 * stages,))],
+        + [block(stages)] * 2
+        + [
+            pltpu.VMEM((MOST_WIN,) + slots[2:], bf16),
+            pltpu.VMEM(slots, bf16),
+            pltpu.VMEM(slots, bf16),
+            pltpu.VMEM((2, caplen, inner), bf16),
+            pltpu.VMEM(w_query.shape, bf16),
+            pltpu.VMEM(w_output.shape, bf16),
+            dma((2 * stages,)),
+            dma((2 * stages,)),
+            dma((n_dev,)),
+            dma((n_dev,)),
+            dma((2,)),
+            dma((2,)),
+        ],
         compiler_params=pltpu.CompilerParams(
-            collective_id=0, has_side_effects=True, vmem_limit_bytes=32 * 1024 * 1024
-        ),
-        cost_estimate=pl.CostEstimate(
-            flops=0, bytes_accessed=64 * 1024 * 1024, transcendentals=0
-        ),
-        name="reduce_rows",
-    )(*(v.reshape((2,) * stages + (rows, width)) for v in (a, b)))
+            collective_id=0, has_side_effects=True, vmem_limit_bytes=48 * 1024 * 1024
+        ),
+        name="tail",
+    )(
+        return_index, target, half, d_kv, memory_kv, part, x, grad_out,
+        gain.reshape(1, model), w_query, w_output,
+    )
 
 
 def swap(x):
@@ -409,39 +565,20 @@
     peer = jnp.concatenate([peer[..., caplen:], peer[..., :caplen]], axis=-1)
     partial, d_kv = attention_grads(live, both[0], both[1], key_value, stats, peer)
 
-    d_memory = (
-        dot(d_kv[0], memory_kv[:, :inner], NT) + dot(d_kv[1], memory_kv[:, inner:], NT)
-    ).astype(jnp.bfloat16)
-    ones = jnp.ones_like(slot_index)
-    grad_slots = gather(return_index, ones, d_memory.reshape(MOST_WIN, tokens, width))
-    returned = lax.all_to_all(
-        grad_slots.reshape(videos, per_slot, tokens, width),
-        "dev",
-        split_axis=0,
-        concat_axis=0,
-        tiled=True,
-    ).reshape(videos * per_slot, tokens, width)
-    memory_grad = gather(target, jnp.ones_like(target), returned)
-
-    terms = [dot(memory_half, d_kv[n], TN).astype(jnp.bfloat16) for n in range(2)]
-    *terms, _ = lax.optimization_barrier((*terms, grad_slots))
-    kv_grad = reduce_rows(*terms)
-
-    other = swap(partial[:, caplen:])
-    merged = (
-        partial[:, :caplen].astype(jnp.float32) + other.astype(jnp.float32)
-    ).astype(jnp.bfloat16)
-    decoded = (x + dot(merged[0], w_output)).astype(jnp.bfloat16)
-    d_scaled = dot(merged[1], w_query, NT) * caption_gain
-    caption_grad = grad_out.astype(jnp.float32) + inv_rms * (
-        d_scaled - x * inv_rms * inv_rms * jnp.mean(d_scaled * x, axis=-1, keepdims=True)
-    )
-    return (
-        decoded[None, None],
-        caption_grad.astype(jnp.bfloat16)[None, None],
-        memory_grad,
-        kv_grad,
-    )
+    kv_grad, memory_grad, decoded, caption_grad = tail(
+        return_index,
+        target,
+        memory_half,
+        d_kv,
+        memory_kv,
+        partial,
+        captions[0, 0],
+        grad_out,
+        caption_gain,
+        w_query,
+        w_output,
+    )
+    return decoded[None, None], caption_grad[None, None], memory_grad, kv_grad
 
 
 def solution(mesh):

time: 184 us -> 173 us (0.940)
  Pallas kernels: 88.3 us -> 101 us
  starting transfers between devices: 23 us -> 10.6 us
  matrix products: 21.7 us -> 10.1 us
  local copies, waits for them, and re-layouts: 10.4 us -> 14.1 us
  waiting for transfers between devices: 32.1 us -> 29.2 us
    pallas_call x1, Pallas kernels: 53.3 us -> 70.1 us  [tail(): pl.pallas_call(functools.partial(tail_kernel, bits), out_shape=[jax.Shape...]
    dot_general x9 -> x3, matrix products: 21.7 us -> 10.1 us  [dot(): return lax.dot_general(a, b, dims, preferred_element_type=jnp.float32)]
    all_to_all x1 -> x0, starting transfers between devices: 10.8 us -> none  [local(): lax.all_to_all(grad_slots.reshape(videos, per_slot, tokens, width), 'dev'...]
    pallas_call x3 -> x1, Pallas kernels: 4.87 us -> 0.81 us  [gather(): pl.pallas_call(gather_kernel, grid_spec=pltpu.PrefetchScalarGridSpec(num_...]
    unnamed x43 -> x30, local copies, waits for them, and re-layouts: 7.24 us -> 11.1 us
    all_to_all x1, waiting for transfers between devices: 19.6 us -> 15.9 us  [local(): lax.all_to_all(packed.reshape(videos, per_slot, tokens, width), 'dev', sp...]
    ppermute x3 -> x2, starting transfers between devices: 4.68 us -> 3.04 us  [swap(): return lax.ppermute(x, 'section', [(0, 1), (1, 0)])]
    ppermute x3 -> x2, waiting for transfers between devices: 12.4 us -> 13.3 us  [swap(): return lax.ppermute(x, 'section', [(0, 1), (1, 0)])]
  transfers between devices with their start and end apart: 5 -> 3, of which waited for: 3 -> 3; matrix products, arithmetic and copies ran while one was open for 11% -> 7% of each run, Pallas kernels for 29% -> 0%
where the time goes in v2:
time: 173 us; the launch traced here: 172 us
  Pallas kernels  101 us (58%)
  waiting for transfers between devices  29.2 us (17%)
  local copies, waits for them, and re-layouts  14.1 us (8%)
  starting transfers between devices  10.6 us (6%)
  matrix products  10.1 us (6%)
  other arithmetic  5.26 us (3%)
  between operations  2.18 us (1%)
    pallas_call x1, Pallas kernels, tail(): pl.pallas_call(functools.partial(tail_kernel, bits), out_shape=[jax.Shape...  70.1 us
    all_to_all x1, waiting for transfers between devices, local(): lax.all_to_all(packed.reshape(videos, per_slot, tokens, width), 'dev', sp...  15.9 us
    ppermute x2, waiting for transfers between devices, swap(): return lax.ppermute(x, 'section', [(0, 1), (1, 0)])  13.3 us
    pallas_call x1, Pallas kernels, attention_grads(): pl.pallas_call(grads_kernel, grid_spec=pltpu.PrefetchScalarGridSpec(num_s...  13.2 us
    unnamed x30, local copies, waits for them, and re-layouts  11.1 us
    dot_general x3, matrix products, dot(): return lax.dot_general(a, b, dims, preferred_element_type=jnp.float32)  10.1 us
    pallas_call x1, Pallas kernels, compress(): pl.pallas_call(compress_kernel, grid_spec=pltpu.PrefetchScalarGridSpec(nu...  9.77 us
    all_to_all x1, starting transfers between devices, local(): lax.all_to_all(packed.reshape(videos, per_slot, tokens, width), 'dev', sp...  7.55 us
  transfers between devices with their start and end apart: 3, of which 3 were waited for; matrix products, arithmetic and copies ran while one was open for 7% of the time, Pallas kernels for 0%

profile of v2, /device:TPU:0, one launch (start us, length us, event | category | flops | bytes accessed | tf_op | source)
XLA Modules:
  0.0 172.5 jit_solution(8011568426299035996)
XLA Ops:
  1.9 1.6 copy-done.6
  3.5 1.2 copy-done.7
  4.7 0.8 copy-done.8
  6.2 9.8 %compress.1 = bf16[32,32,1024]{2,1,0:T(8,128)(2,1)S(1)} custom-call(s32[32]{0:T(128)S(1)} %select_reduce_fusion.1.index_ref, bf16[16,32,1024]{2,1,0:T(8,128)(2,1)S(1)} %copy-done.7, bf16[32,1024]{1,0:T(8,128)(2,1)S(1)} %copy-done.8, bf16[1024,2048]{1,0:T(8,128)(2,1)} %kv_ref.1, bf16[1024,1024]{1,0:T(8,128)(2,1)S(1)} %copy-done.6, f32[1,1024]{1,0:T(1,128)S(1)} %bitcast.45), custom_call_target="tpu_custom_call" | custom-call | flops 4294967296 | bytes 12582912 | tf_op jit(solution)/shard_map/compress/pallas_call | solution.py:75
  16.0 1.3 copy-done.4
  17.3 7.6 %all-to-all-start = ((bf16[16,2,32,1024]{3,2,1,0:T(8,128)(2,1)}), bf16[16,2,32,1024]{3,2,1,0:T(8,128)(2,1)S(1)}, u32[]{:S(2)}, u32[]{:S(2)}) async-start(bf16[16,2,32,1024]{3,2,1,0:T(8,128)(2,1)} %bitcast.41), calls=%async_computation | async-start | bytes 4194304 | tf_op jit(solution)/shard_map/all_to_all | solution.py:555
  25.8 1.2 bitcast_select_fusion.grad_out_ref
  26.9 3.9 %fusion.1 = bf16[1,128,1024]{2,1,0:T(8,128)(2,1)S(1)} fusion(bf16[128,2048]{1,0:T(8,128)(2,1)S(1)} %bitcast_select_fusion.grad_out_ref, bf16[1024,2048]{1,0:T(8,128)(2,1)} %w_output_ref.1), kind=kOutput, calls=%fused_computation.6 | convolution fusion | flops 537001984 | bytes 4980736 | tf_op jit(solution)/shard_map/dot_general | solution.py:20
  30.8 0.8 fusion
  32.3 0.8 pad_maximum_fusion.1
  33.2 1.5 collective-permute-start
  37.8 9.9 %collective-permute-done = bf16[2,128,1024]{2,1,0:T(8,128)(2,1)} collective-permute-done((bf16[2,128,1024]{2,1,0:T(8,128)(2,1)}, bf16[2,128,1024]{2,1,0:T(8,128)(2,1)}, u32[]{:S(2)}, u32[]{:S(2)}) %collective-permute-start) | collective-permute-done | bytes 524320 | tf_op jit(solution)/shard_map/ppermute | solution.py:491
  47.7 1.2 pad_maximum_fusion
  48.9 1.0 slice_bitcast_fusion
  50.0 15.9 %all-to-all-done = bf16[16,2,32,1024]{3,2,1,0:T(8,128)(2,1)S(1)} async-done(((bf16[16,2,32,1024]{3,2,1,0:T(8,128)(2,1)}), bf16[16,2,32,1024]{3,2,1,0:T(8,128)(2,1)S(1)}, u32[]{:S(2)}, u32[]{:S(2)}) %all-to-all-start) | async-done | bytes 2097184 | tf_op jit(solution)/shard_map/all_to_all | solution.py:555
  65.9 0.8 gather.1
  66.7 5.4 %convolution_convert_fusion.k_ref.v_ref = bf16[640,2048]{1,0:T(8,128)(2,1)S(1)} fusion(bf16[640,1024]{1,0:T(8,128)(2,1)S(1)} %bitcast.38, bf16[1024,2048]{1,0:T(8,128)(2,1)} %memory_kv_ref.1), kind=kOutput, calls=%fused_computation | convolution fusion | flops 2685665280 | bytes 8126464 | tf_op jit(solution)/shard_map/dot_general | solution.py:20
  72.1 7.2 %attention_stats.1.mine_ref = f32[8,8,256]{2,1,0:T(8,128)S(1)} custom-call(s32[1]{0:T(128)} %bitcast.8.live_ref, bf16[256,1024]{1,0:T(8,128)(2,1)S(1)} %copy-done.2, bf16[256,1024]{1,0:T(8,128)(2,1)S(1)} %copy-done.1, bf16[640,2048]{1,0:T(8,128)(2,1)S(1)} %convolution_convert_fusion.k_ref.v_ref, bf16[640,2048]{1,0:T(8,128)(2,1)S(1)} %convolution_convert_fusion.k_ref.v_ref), custom_call_target="tpu_custom_call" | custom-call | tf_op jit(solution)/shard_map/attention_stats/pallas_call | solution.py:199
  79.4 1.6 collective-permute-start.1
  81.0 3.4 %collective-permute-done.1 = f32[8,8,256]{2,1,0:T(8,128)S(1)} collective-permute-done((f32[8,8,256]{2,1,0:T(8,128)S(1)}, f32[8,8,256]{2,1,0:T(8,128)S(1)}, u32[]{:S(2)}, u32[]{:S(2)}) %collective-permute-start.1) | collective-permute-done | bytes 65568 | tf_op jit(solution)/shard_map/ppermute | solution.py:491
  84.4 13.2 %attention_grads.1 = (bf16[2,256,1024]{2,1,0:T(8,128)(2,1)S(1)}, bf16[2,640,1024]{2,1,0:T(8,128)(2,1)S(1)}) custom-call(s32[1]{0:T(128)} %bitcast.8.live_ref, bf16[256,1024]{1,0:T(8,128)(2,1)S(1)} %copy-done.2, bf16[256,1024]{1,0:T(8,128)(2,1)S(1)} %copy-done.1, bf16[640,2048]{1,0:T(8,128)(2,1)S(1)} %convolution_convert_fusion.k_ref.v_ref, ...), custom_call_target="tpu_custom_call" | custom-call | tf_op jit(solution)/shard_map/attention_grads/pallas_call | solution.py:218
  97.6 1.5 copy-done.3
  99.1 70.1 %tail.1 = (f32[32,2048]{1,0:T(8,128)S(1)}, bf16[16,32,1024]{2,1,0:T(8,128)(2,1)S(1)}, bf16[128,2048]{1,0:T(8,128)(2,1)S(1)}, bf16[128,2048]{1,0:T(8,128)(2,1)S(1)}) custom-call(s32[32]{0:T(128)S(1)} %select_reduce_fusion.return_ref, s32[16]{0:T(128)S(1)} %multiply_add_fusion.target_ref, bf16[640,1024]{1,0:T(8,128)(2,1)S(1)} %bitcast.39, ...), custom_call_target="tpu_custom_call" | custom-call | tf_op jit(solution)/shard_map/tail/pallas_call | solution.py:453
  170.8 1.0 copy.27
  (43 shorter events, 7.7 us)
Async XLA Ops:
  1.9 1.6 copy-start.6
  3.5 1.2 copy-start.7
  4.7 0.8 copy-start.8
  5.5 0.7 copy-start.9
  16.0 1.3 copy-start.4
  17.3 8.2 %copy-start = (bf16[1,1,128,2048]{3,2,1,0:T(8,128)(2,1)S(1)}, bf16[1,1,128,2048]{3,2,1,0:T(8,128)(2,1)}, u32[]{:S(2)}) copy-start(bf16[1,1,128,2048]{3,2,1,0:T(8,128)(2,1)} %param.19) | copy-start | bytes 1572868
  17.3 48.5 %all-to-all-start = ((bf16[16,2,32,1024]{3,2,1,0:T(8,128)(2,1)}), bf16[16,2,32,1024]{3,2,1,0:T(8,128)(2,1)S(1)}, u32[]{:S(2)}, u32[]{:S(2)}) async-start(bf16[16,2,32,1024]{3,2,1,0:T(8,128)(2,1)} %bitcast.41), calls=%async_computation | async-start | bytes 4194304 | tf_op jit(solution)/shard_map/all_to_all | solution.py:555
  26.9 3.9 %copy-start.5 = (f32[2048]{0:T(1024)S(1)}, f32[2048]{0:T(1024)}, u32[]{:S(2)}) copy-start(f32[2048]{0:T(1024)} %param.21) | copy-start | bytes 24580
  26.9 3.9 %copy-start.10 = (bf16[2048,1024]{1,0:T(8,128)(2,1)S(1)}, bf16[2048,1024]{1,0:T(8,128)(2,1)}, u32[]{:S(2)}) copy-start(bf16[2048,1024]{1,0:T(8,128)(2,1)} %w_query_ref.1) | copy-start | bytes 12582916
  30.8 3.9 %copy-start.12 = (s32[2,16]{1,0:T(2,128)S(1)}, s32[2,16]{1,0:T(2,128)}, u32[]{:S(2)}) copy-start(s32[2,16]{1,0:T(2,128)} %param.14) | copy-start | bytes 388
  31.6 0.7 copy-start.11
  33.2 14.6 %collective-permute-start = (bf16[2,128,1024]{2,1,0:T(8,128)(2,1)}, bf16[2,128,1024]{2,1,0:T(8,128)(2,1)}, u32[]{:S(2)}, u32[]{:S(2)}) collective-permute-start(bf16[2,128,1024]{2,1,0:T(8,128)(2,1)} %pad_maximum_fusion.1), channel_id=1, source_target_pairs={{0,16},{16,0},{1,17},{17,1},{2,18},{18,2},{3,19},{19,3},{4,20},{20... | collective-permute-start | bytes 1572872 | tf_op jit(solution)/shard_map/ppermute | solution.py:491
  66.7 5.4 %copy-start.1 = (bf16[256,1024]{1,0:T(8,128)(2,1)S(1)}, bf16[256,1024]{1,0:T(8,128)(2,1)}, u32[]{:S(2)}) copy-start(bf16[256,1024]{1,0:T(8,128)(2,1)} %get-tuple-element.16.g_ref) | copy-start | bytes 1572868
  66.7 5.4 %copy-start.2 = (bf16[256,1024]{1,0:T(8,128)(2,1)S(1)}, bf16[256,1024]{1,0:T(8,128)(2,1)}, u32[]{:S(2)}) copy-start(bf16[256,1024]{1,0:T(8,128)(2,1)} %get-tuple-element.17.q_ref) | copy-start | bytes 1572868
  79.4 5.0 %collective-permute-start.1 = (f32[8,8,256]{2,1,0:T(8,128)S(1)}, f32[8,8,256]{2,1,0:T(8,128)S(1)}, u32[]{:S(2)}, u32[]{:S(2)}) collective-permute-start(f32[8,8,256]{2,1,0:T(8,128)S(1)} %attention_stats.1.mine_ref), channel_id=1, source_target_pairs={{0,16},{16,0},{1,17},{17,1},{2,18},{18,2},{3,19},{19,3},{4,20},{20... | collective-permute-start | bytes 196616 | tf_op jit(solution)/shard_map/ppermute | solution.py:491
  97.6 1.5 copy-start.3

commit v3 on v2

--- a/solution.py
+++ b/solution.py
@@ -25,107 +25,189 @@
     return jnp.where(lane // HEAD_DIM == which, x, jnp.zeros_like(x))
 
 
-def compress_kernel(
-    index_ref, frames_ref, queries_ref, kv_ref, out_w_ref, gain_ref, packed_ref, kv_s, ctx_s, mem_s
+def head_kernel(
+    send_ref, source_ref, frames_ref, queries_ref, frame_kv_ref, query_out_ref, gain_ref,
+    normed_ref, grad_out_ref, w_query_ref, w_output_ref, memory_kv_ref,
+    both_ref, half_ref, keys_ref,
+    kv_s, ctx_s, mem_s, slots, arrived, own, swapped, w_query_s, w_output_s, memory_kv_s,
+    slot_send, slot_recv, swap_sem, load_sem,
 ):
-    step = pl.program_id(0)
-    group, frames, width = frames_ref.shape
+    mesh_ids = pl.DeviceIdType.MESH
+    section, dev = lax.axis_index("section"), lax.axis_index("dev")
+    n_dev, per_slot = slots.shape[:2]
+    loads = [
+        pltpu.make_async_copy(src, dst, load_sem.at[n])
+        for n, (src, dst) in enumerate(
+            ((w_query_ref, w_query_s), (w_output_ref, w_output_s), (memory_kv_ref, memory_kv_s))
+        )
+    ]
+    for load in loads:
+        load.start()
+    barrier = pltpu.get_barrier_semaphore()
+    peer = (1 - section, dev)
+    pl.semaphore_signal(barrier, inc=1, device_id=peer, device_id_type=mesh_ids)
+
+    def greet(k, carry):
+        to = (section, lax.rem(dev + k, n_dev))
+        pl.semaphore_signal(barrier, inc=1, device_id=to, device_id_type=mesh_ids)
+        return carry
+
+    lax.fori_loop(1, n_dev, greet, 0)
+    windows, frames, width = frames_ref.shape
     tokens = queries_ref.shape[0]
-    kv_s[...] = dot(frames_ref[...].reshape(group * frames, width), kv_ref[...]).astype(jnp.bfloat16)
-    heads = 4
-    span = heads * HEAD_DIM
-    lane = lax.broadcasted_iota(jnp.int32, (tokens, span), 1) // HEAD_DIM
-    for part in range(width // span):
-        lo = part * span
-        queries = queries_ref[:, lo : lo + span]
-        stacked = jnp.concatenate(
-            [jnp.where(lane == h, queries, jnp.zeros_like(queries)) for h in range(heads)], axis=0
+    group = kv_s.shape[0] // frames
+
+    def compress(step, carry):
+        block = frames_ref[pl.ds(step * group, group)].reshape(group * frames, width)
+        kv_s[...] = dot(block, frame_kv_ref[...]).astype(jnp.bfloat16)
+        heads = 4
+        span = heads * HEAD_DIM
+        lane = lax.broadcasted_iota(jnp.int32, (tokens, span), 1) // HEAD_DIM
+        for part in range(width // span):
+            lo = part * span
+            queries = queries_ref[:, lo : lo + span]
+            stacked = jnp.concatenate(
+                [jnp.where(lane == h, queries, jnp.zeros_like(queries)) for h in range(heads)], axis=0
+            )
+            scores = dot(kv_s[:, lo : lo + span], stacked, NT) * SCALE
+            scores = scores.reshape(group, frames, heads * tokens)
+            weights = jnp.exp(scores - jnp.max(scores, axis=1, keepdims=True))
+            weights = (weights / jnp.sum(weights, axis=1, keepdims=True)).astype(jnp.bfloat16)
+            for w in range(group):
+                rows = slice(w * frames, (w + 1) * frames)
+                every = dot(weights[w], kv_s[rows, width + lo : width + lo + span], TN)
+                mixed = every[:tokens]
+                for h in range(1, heads):
+                    mixed = jnp.where(lane == h, every[h * tokens : (h + 1) * tokens], mixed)
+                ctx_s[w * tokens : (w + 1) * tokens, lo : lo + span] = mixed.astype(jnp.bfloat16)
+        projected = dot(ctx_s[...], query_out_ref[...]).reshape(group, tokens, width)
+        hidden = queries_ref[...].astype(jnp.float32)[None] + projected
+        scale = lax.rsqrt(jnp.mean(hidden * hidden, axis=-1, keepdims=True) + EPSILON)
+        memory = hidden * scale * gain_ref[...][None]
+        mem_s[pl.ds(step * group, group)] = memory.astype(jnp.bfloat16)
+        return carry
+
+    lax.fori_loop(0, windows // group, compress, 0)
+
+    def pack(i, carry):
+        slots[i // per_slot, lax.rem(i, per_slot)] = mem_s[send_ref[i]]
+        return carry
+
+    lax.fori_loop(0, n_dev * per_slot, pack, 0)
+    pl.semaphore_wait(barrier, n_dev)
+
+    def slot_copy(k):
+        to = lax.rem(dev + k, n_dev)
+        return pltpu.make_async_remote_copy(
+            src_ref=slots.at[to],
+            dst_ref=arrived.at[dev],
+            send_sem=slot_send.at[k],
+            recv_sem=slot_recv.at[k],
+            device_id=(section, to),
+            device_id_type=mesh_ids,
         )
-        scores = dot(kv_s[:, lo : lo + span], stacked, NT) * SCALE
-        scores = scores.reshape(group, frames, heads * tokens)
-        weights = jnp.exp(scores - jnp.max(scores, axis=1, keepdims=True))
-        weights = (weights / jnp.sum(weights, axis=1, keepdims=True)).astype(jnp.bfloat16)
-        for w in range(group):
-            rows = slice(w * frames, (w + 1) * frames)
-            every = dot(weights[w], kv_s[rows, width + lo : width + lo + span], TN)
-            mixed = every[:tokens]
-            for h in range(1, heads):
-                mixed = jnp.where(lane == h, every[h * tokens : (h + 1) * tokens], mixed)
-            ctx_s[w * tokens : (w + 1) * tokens, lo : lo + span] = mixed.astype(jnp.bfloat16)
-    projected = dot(ctx_s[...], out_w_ref[...]).reshape(group, tokens, width)
-    hidden = queries_ref[...].astype(jnp.float32)[None] + projected
-    scale = lax.rsqrt(jnp.mean(hidden * hidden, axis=-1, keepdims=True) + EPSILON)
-    mem_s[pl.ds(step * group, group)] = (hidden * scale * gain_ref[...][None]).astype(jnp.bfloat16)
-
-    @pl.when(step == pl.num_programs(0) - 1)
-    def _():
-        def place(slot, carry):
-            packed_ref[slot] = mem_s[index_ref[slot]]
-            return carry
-
-        lax.fori_loop(0, packed_ref.shape[0], place, 0)
-
-
-def compress(index, frames, queries, frame_kv, query_out, gain):
+
+    def send_slot(i, carry):
+        slot_copy(lax.rem(i + n_dev // 2 - 1, n_dev - 1) + 1).start()
+        return carry
+
+    lax.fori_loop(0, n_dev - 1, send_slot, 0)
+    arrived[dev] = slots[dev]
+    for load in loads:
+        load.wait()
+    caplen = normed_ref.shape[0]
+    own[0] = dot(normed_ref[...], w_query_s[...]).astype(jnp.bfloat16)
+    own[1] = dot(grad_out_ref[...], w_output_s[...], NT).astype(jnp.bfloat16)
+    both_ref[:, :caplen, :] = own[...]
+    swap_copy = pltpu.make_async_remote_copy(
+        src_ref=own,
+        dst_ref=swapped,
+        send_sem=swap_sem.at[0],
+        recv_sem=swap_sem.at[1],
+        device_id=peer,
+        device_id_type=mesh_ids,
+    )
+    swap_copy.start()
+    swap_copy.wait_recv()
+    both_ref[:, caplen:, :] = swapped[...]
+
+    def arrive(k, carry):
+        slot_copy(k).wait_recv()
+        return carry
+
+    lax.fori_loop(1, n_dev, arrive, 0)
+
+    def take(p, carry):
+        at = source_ref[p]
+        rows = pl.ds(pl.multiple_of(p * tokens, tokens), tokens)
+        half_ref[rows, :] = arrived[at // per_slot, lax.rem(at, per_slot)]
+        return carry
+
+    lax.fori_loop(0, half_ref.shape[0] // tokens, take, 0)
+    chunk = memory_kv_s.shape[1] // 4
+
+    def project(j, carry):
+        at = pl.ds(pl.multiple_of(j * chunk, chunk), chunk)
+        keys_ref[:, at] = dot(half_ref[...], memory_kv_s[:, at]).astype(jnp.bfloat16)
+        return carry
+
+    lax.fori_loop(0, 4, project, 0)
+
+    def sent(k, carry):
+        slot_copy(k).wait_send()
+        return carry
+
+    lax.fori_loop(1, n_dev, sent, 0)
+    swap_copy.wait_send()
+
+
+def head(
+    send_index, source_slot, frames, queries, frame_kv, query_out, gain,
+    normed, grad_out, w_query, w_output, memory_kv,
+):
+    n_dev = lax.axis_size("dev")
     windows, length, width = frames.shape
     tokens = queries.shape[0]
-    slots = index.shape[0]
+    caplen, inner = normed.shape[0], w_query.shape[1]
+    keys = MOST_WIN * tokens
+    slots = (n_dev, send_index.shape[0] // n_dev, tokens, width)
     group = 8
-    whole = lambda *shape: pl.BlockSpec(shape, lambda i, idx: (0,) * len(shape))
+    bf16 = jnp.bfloat16
+    vmem = pl.BlockSpec(memory_space=pltpu.VMEM)
+    smem = pl.BlockSpec(memory_space=pltpu.SMEM)
+    far = pl.BlockSpec(memory_space=pl.ANY)
+    dma = pltpu.SemaphoreType.DMA
+    shapes = [
+        (group * length, 2 * width),
+        (group * tokens, width),
+        (windows, tokens, width),
+        slots,
+        slots,
+        (2, caplen, inner),
+        (2, caplen, inner),
+        w_query.shape,
+        w_output.shape,
+        memory_kv.shape,
+    ]
     return pl.pallas_call(
-        compress_kernel,
-        grid_spec=pltpu.PrefetchScalarGridSpec(
-            num_scalar_prefetch=1,
-            grid=(windows // group,),
-            in_specs=[
-                pl.BlockSpec((group, length, width), lambda i, idx: (i, 0, 0)),
-                whole(tokens, width),
-                whole(width, 2 * width),
-                whole(width, width),
-                whole(1, width),
-            ],
-            out_specs=whole(slots, tokens, width),
-            scratch_shapes=[
-                pltpu.VMEM((group * length, 2 * width), jnp.bfloat16),
-                pltpu.VMEM((group * tokens, width), jnp.bfloat16),
-                pltpu.VMEM((windows, tokens, width), jnp.bfloat16),
-            ],
+        head_kernel,
+        out_shape=[
+            jax.ShapeDtypeStruct((2, 2 * caplen, inner), bf16),
+            jax.ShapeDtypeStruct((keys, width), bf16),
+            jax.ShapeDtypeStruct((keys, memory_kv.shape[1]), bf16),
+        ],
+        in_specs=[smem] * 2 + [vmem] * 7 + [far] * 3,
+        out_specs=[vmem] * 3,
+        scratch_shapes=[pltpu.VMEM(shape, bf16) for shape in shapes]
+        + [dma((n_dev,)), dma((n_dev,)), dma((2,)), dma((3,))],
+        compiler_params=pltpu.CompilerParams(
+            collective_id=1, has_side_effects=True, vmem_limit_bytes=40 * 1024 * 1024
         ),
-        out_shape=jax.ShapeDtypeStruct((slots, tokens, width), jnp.bfloat16),
-        compiler_params=pltpu.CompilerParams(vmem_limit_bytes=48 * 1024 * 1024),
-        cost_estimate=pl.CostEstimate(
-            flops=2 * windows * length * width * width * 4,
-            bytes_accessed=12 * 1024 * 1024,
-            transcendentals=0,
-        ),
-        name="compress",
-    )(index, frames, queries, frame_kv, query_out, gain.reshape(1, width))
-
-
-def gather_kernel(index_ref, live_ref, table_ref, out_ref):
-    def place(row, carry):
-        value = table_ref[index_ref[row]]
-        out_ref[row] = jnp.where(live_ref[row] > 0, value, jnp.zeros_like(value))
-        return carry
-
-    lax.fori_loop(0, out_ref.shape[0], place, 0)
-
-
-def gather(index, live, table):
-    rows = index.shape[0]
-    shape = (rows,) + table.shape[1:]
-    return pl.pallas_call(
-        gather_kernel,
-        grid_spec=pltpu.PrefetchScalarGridSpec(
-            num_scalar_prefetch=2,
-            grid=(1,),
-            in_specs=[pl.BlockSpec(table.shape, lambda i, a, b: (0, 0, 0))],
-            out_specs=pl.BlockSpec(shape, lambda i, a, b: (0, 0, 0)),
-        ),
-        out_shape=jax.ShapeDtypeStruct(shape, table.dtype),
-        compiler_params=pltpu.CompilerParams(vmem_limit_bytes=24 * 1024 * 1024),
-        name="gather",
-    )(index, live, table)
+        name="head",
+    )(
+        send_index, source_slot, frames, queries, frame_kv, query_out, gain.reshape(1, width),
+        normed, grad_out, w_query, w_output, memory_kv,
+    )
 
 
 def masked_scores(keys, queries, live):
@@ -544,21 +626,22 @@
     x = captions[0, 0].astype(jnp.float32)
     inv_rms = lax.rsqrt(jnp.mean(x * x, axis=-1, keepdims=True) + EPSILON)
     normed = (x * inv_rms * caption_gain).astype(jnp.bfloat16)
-    query = dot(normed, w_query).astype(jnp.bfloat16)
     row_live = jnp.arange(caplen, dtype=jnp.int32) < caption_lengths[0, 0]
     grad_out = jnp.where(row_live[:, None], upstream[0, 0], jnp.zeros_like(upstream[0, 0]))
-    d_context = dot(grad_out, w_output, NT).astype(jnp.bfloat16)
-    own = jnp.stack([query, d_context])
-    both = jnp.concatenate([own, swap(own)], axis=1)
-
-    packed = compress(send_index, frames, learned_queries, frame_kv, query_out, query_gain)
-    arrived = lax.all_to_all(
-        packed.reshape(videos, per_slot, tokens, width), "dev", split_axis=0, concat_axis=0, tiled=True
-    ).reshape(videos * per_slot, tokens, width)
-    memory_half = gather(source_slot, present.astype(jnp.int32), arrived).reshape(
-        MOST_WIN * tokens, width
-    )
-    key_value = dot(memory_half, memory_kv).astype(jnp.bfloat16)
+    both, memory_half, key_value = head(
+        send_index,
+        source_slot,
+        frames,
+        learned_queries,
+        frame_kv,
+        query_out,
+        query_gain,
+        normed,
+        grad_out,
+        w_query,
+        w_output,
+        memory_kv,
+    )
 
     stats = attention_stats(live, both[0], both[1], key_value)
     peer = swap(stats)

time: 173 us -> 174 us (level)
  Pallas kernels: 101 us -> 144 us
  waiting for transfers between devices: 29.2 us -> 2.07 us
  matrix products: 10.1 us -> 0 us
  starting transfers between devices: 10.6 us -> 1.58 us
  local copies, waits for them, and re-layouts: 14.1 us -> 17.4 us
    pallas_call x2 -> x1, Pallas kernels: 10.6 us -> 61 us  [head(): pl.pallas_call(head_kernel, out_shape=[jax.ShapeDtypeStruct((2, 2 * caple...]
    all_to_all x1 -> x0, waiting for transfers between devices: 15.9 us -> none  [local(): lax.all_to_all(packed.reshape(videos, per_slot, tokens, width), 'dev', sp...]
    ppermute x2 -> x1, waiting for transfers between devices: 13.3 us -> 2.07 us  [swap(): return lax.ppermute(x, 'section', [(0, 1), (1, 0)])]
    dot_general x3 -> x0, matrix products: 10.1 us -> none  [dot(): return lax.dot_general(a, b, dims, preferred_element_type=jnp.float32)]
    all_to_all x1 -> x0, starting transfers between devices: 7.55 us -> none  [local(): lax.all_to_all(packed.reshape(videos, per_slot, tokens, width), 'dev', sp...]
    pallas_call x1, Pallas kernels: 70.1 us -> 63.1 us  [tail(): pl.pallas_call(functools.partial(tail_kernel, bits), out_shape=[jax.Shape...]
    unnamed x30, local copies, waits for them, and re-layouts: 11.1 us -> 14.5 us
  transfers between devices with their start and end apart: 3 -> 1, of which waited for: 3 -> 1; matrix products, arithmetic and copies ran while one was open for 7% -> 0% of each run, Pallas kernels for 0% -> 0%
where the time goes in v3:
time: 174 us
  Pallas kernels  144 us (83%)
  local copies, waits for them, and re-layouts  17.4 us (10%)
  other arithmetic  6.18 us (4%)
  between operations  2.09 us (1%)
  waiting for transfers between devices  2.07 us (1%)
    pallas_call x1, Pallas kernels, tail(): pl.pallas_call(functools.partial(tail_kernel, bits), out_shape=[jax.Shape...  63.1 us
    pallas_call x1, Pallas kernels, head(): pl.pallas_call(head_kernel, out_shape=[jax.ShapeDtypeStruct((2, 2 * caple...  61 us
    unnamed x30, local copies, waits for them, and re-layouts  14.5 us
    pallas_call x1, Pallas kernels, attention_grads(): pl.pallas_call(grads_kernel, grid_spec=pltpu.PrefetchScalarGridSpec(num_s...  13.2 us
    pallas_call x1, Pallas kernels, attention_stats(): pl.pallas_call(stats_kernel, grid_spec=pltpu.PrefetchScalarGridSpec(num_s...  7.21 us
  transfers between devices with their start and end apart: 1, of which 1 were waited for; matrix products, arithmetic and copies ran while one was open for 0% of the time, Pallas kernels for 0%

profile of v3, /device:TPU:0, one launch (start us, length us, event | category | flops | bytes accessed | tf_op | source)
XLA Modules:
  0.0 173.8 jit_solution(14561842309885683213)
XLA Ops:
  1.3 0.7 fusion.10
  2.0 1.2 fusion
  3.5 0.7 bitcast_subtract_fusion
  5.7 1.1 bitcast_select_fusion.grad_out_ref
  6.9 1.2 fusion.2.normed_ref
  8.1 2.2 %copy-done.3 = bf16[1024,2048]{1,0:T(8,128)(2,1)S(1)} copy-done((bf16[1024,2048]{1,0:T(8,128)(2,1)S(1)}, bf16[1024,2048]{1,0:T(8,128)(2,1)}, u32[]{:S(2)}) %copy-start.3) | copy-done | bytes 4194328
  10.3 1.6 copy-done.5
  11.9 1.2 copy-done.8
  13.1 0.8 copy-done.9
  14.6 61.0 %head.1 = (bf16[2,256,1024]{2,1,0:T(8,128)(2,1)S(1)}, bf16[640,1024]{1,0:T(8,128)(2,1)S(1)}, bf16[640,2048]{1,0:T(8,128)(2,1)S(1)}) custom-call(s32[32]{0:T(128)S(1)} %select_reduce_fusion.1.send_ref, s32[20]{0:T(128)S(1)} %fusion.4.source_ref, bf16[16,32,1024]{2,1,0:T(8,128)(2,1)S(1)} %copy-done.8, bf16[32,1024]{1,0:T(8,128)(2,1)S(1)} %copy-done.9, ...), custom_call_target="tpu_custom_call" | custom-call | tf_op jit(solution)/shard_map/head/pallas_call | solution.py:192
  75.6 1.1 copy-done.6
  76.7 1.0 slice_bitcast_fusion
  79.0 1.0 copy-done.1
  80.0 1.0 copy-done.2
  81.1 7.2 %attention_stats.1.mine_ref = f32[8,8,256]{2,1,0:T(8,128)S(1)} custom-call(s32[1]{0:T(128)} %bitcast.8.live_ref, bf16[256,1024]{1,0:T(8,128)(2,1)S(1)} %copy-done.2, bf16[256,1024]{1,0:T(8,128)(2,1)S(1)} %copy-done.1, bf16[640,2048]{1,0:T(8,128)(2,1)S(1)} %get-tuple-element.15.k_ref.v_ref, bf16[640,2048]{1,0:T(8,128)(2,1)S(1)} %get-tuple-element.15.k_ref.v_ref), custom_call_target="tpu_custom_call" | custom-call | tf_op jit(solution)/shard_map/attention_stats/pallas_call | solution.py:281
  88.3 1.6 collective-permute-start
  90.6 2.1 %collective-permute-done = f32[8,8,256]{2,1,0:T(8,128)S(1)} collective-permute-done((f32[8,8,256]{2,1,0:T(8,128)S(1)}, f32[8,8,256]{2,1,0:T(8,128)S(1)}, u32[]{:S(2)}, u32[]{:S(2)}) %collective-permute-start) | collective-permute-done | bytes 65568 | tf_op jit(solution)/shard_map/ppermute | solution.py:573
  92.7 13.2 %attention_grads.1 = (bf16[2,256,1024]{2,1,0:T(8,128)(2,1)S(1)}, bf16[2,640,1024]{2,1,0:T(8,128)(2,1)S(1)}) custom-call(s32[1]{0:T(128)} %bitcast.8.live_ref, bf16[256,1024]{1,0:T(8,128)(2,1)S(1)} %copy-done.2, bf16[256,1024]{1,0:T(8,128)(2,1)S(1)} %copy-done.1, bf16[640,2048]{1,0:T(8,128)(2,1)S(1)} %get-tuple-element.15.k_ref.v_ref, ...), custom_call_target="tpu_custom_call" | custom-call | tf_op jit(solution)/shard_map/attention_grads/pallas_call | solution.py:300
  105.9 1.5 copy-done.4
  107.4 63.1 %tail.1 = (f32[32,2048]{1,0:T(8,128)S(1)}, bf16[16,32,1024]{2,1,0:T(8,128)(2,1)S(1)}, bf16[128,2048]{1,0:T(8,128)(2,1)S(1)}, bf16[128,2048]{1,0:T(8,128)(2,1)S(1)}) custom-call(s32[32]{0:T(128)S(1)} %select_reduce_fusion.return_ref, s32[16]{0:T(128)S(1)} %multiply_add_fusion.target_ref, bf16[640,1024]{1,0:T(8,128)(2,1)S(1)} %copy-done.7, ...), custom_call_target="tpu_custom_call" | custom-call | tf_op jit(solution)/shard_map/tail/pallas_call | solution.py:535
  170.5 0.8 copy.25
  171.3 0.8 copy.26
  172.1 1.0 copy.27
  173.1 0.7 copy.28
  (34 shorter events, 3.8 us)
Async XLA Ops:
  8.1 2.2 %copy-start.3 = (bf16[1024,2048]{1,0:T(8,128)(2,1)S(1)}, bf16[1024,2048]{1,0:T(8,128)(2,1)}, u32[]{:S(2)}) copy-start(bf16[1024,2048]{1,0:T(8,128)(2,1)} %frame_kv_ref.1) | copy-start | bytes 12582916
  10.3 1.6 copy-start.5
  11.9 1.2 copy-start.8
  13.1 0.8 copy-start.9
  14.0 0.7 copy-start.11
  14.6 63.1 %copy-start.12 = (s32[2,16]{1,0:T(2,128)S(1)}, s32[2,16]{1,0:T(2,128)}, u32[]{:S(2)}) copy-start(s32[2,16]{1,0:T(2,128)} %param.14) | copy-start | bytes 388
  75.6 1.1 copy-start.6
  79.0 1.0 copy-start.1
  80.0 1.0 copy-start.2
  88.3 19.2 %copy-start = (bf16[1,1,128,2048]{3,2,1,0:T(8,128)(2,1)S(1)}, bf16[1,1,128,2048]{3,2,1,0:T(8,128)(2,1)}, u32[]{:S(2)}) copy-start(bf16[1,1,128,2048]{3,2,1,0:T(8,128)(2,1)} %param.19) | copy-start | bytes 1572868
  88.3 19.1 %copy-start.7 = (bf16[640,1024]{1,0:T(8,128)(2,1)S(1)}, bf16[640,1024]{1,0:T(8,128)(2,1)}, u32[]{:S(2)}) copy-start(bf16[640,1024]{1,0:T(8,128)(2,1)} %copy-done.6) | copy-start | bytes 3932164
  88.3 19.1 %copy-start.10 = (f32[2048]{0:T(1024)S(1)}, f32[2048]{0:T(1024)}, u32[]{:S(2)}) copy-start(f32[2048]{0:T(1024)} %param.21) | copy-start | bytes 24580
  88.3 4.4 %collective-permute-start = (f32[8,8,256]{2,1,0:T(8,128)S(1)}, f32[8,8,256]{2,1,0:T(8,128)S(1)}, u32[]{:S(2)}, u32[]{:S(2)}) collective-permute-start(f32[8,8,256]{2,1,0:T(8,128)S(1)} %attention_stats.1.mine_ref), channel_id=1, source_target_pairs={{0,16},{16,0},{1,17},{17,1},{2,18},{18,2},{3,19},{19,3},{4,20},{20... | collective-permute-start | bytes 196616 | tf_op jit(solution)/shard_map/ppermute | solution.py:573
  105.9 1.5 copy-start.4
